TPU v7x, 256 devices: a whole 4x4x8 slice. The times are simulated.
256 devices in a mesh: dp: 64 (over z_hi, x, y), ctx: 4 (over z_lo, core).
Axes of the slice: x: 4, y: 4, z: 8 (z_hi: 4, z_lo: 2; z = z_hi * 2 + z_lo), core: 2. Of those that a mesh axis runs over, the one named last changes fastest.
Arguments:
- latents: bfloat16 [32768, 2560], P(('dp', 'ctx')), may hold values from -6 to 6
- noise: bfloat16 [32768, 2560], P('dp', 'ctx'), may hold values from -6 to 6
- steps: int32 [64], replicated, may hold values from 0 to 999
- layout: int32 [64, 512], P('dp'), may hold values from 0 to 511, as said below
- w_time: bfloat16 [256, 7680], replicated, may hold values from -0.375 to 0.375
- w_student: bfloat16 [2560, 2560], P('dp', 'ctx'), may hold values from -0.125 to 0.125
- w_qk: bfloat16 [2560, 5120], P('dp', 'ctx'), may hold values from -4 to 4
- w_value: bfloat16 [2560, 2560], P('dp', 'ctx'), may hold values from -0.125 to 0.125
- w_disc: float32 [2560], P('ctx'), may hold values from -3 to 3
Outputs:
- clip_loss: float32 [64], replicated
- student_grad: float32 [2560, 2560], P('dp', 'ctx')
Inputs may be any that keep to these rules, and one draw needn't show every extreme that they name: `layout`: each row holds every position of 0 to 511 once.
All inputs are finite; a program needn't handle non-finite values.
Results may differ from a plain program's by a relative error of at most 0.0059.
Values may be sent and summed in bfloat16 or wider, within the bound.
A program may use at most 128 MiB of HBM per device.

v0:
```python
import math

import jax
import jax.numpy as jnp
from jax import lax
from jax.sharding import PartitionSpec as P

HD = 128
FREQ = 256
STEPS = 1000


ln_eps = 1e-06
exact_dots = lax.Precision.HIGHEST


def normalize(matrix):
    mean_row = jnp.mean(matrix, axis=-1, keepdims=True)
    centered = matrix - mean_row
    inverse = lax.rsqrt(jnp.mean(centered * centered, axis=-1, keepdims=True) + ln_eps)
    return (centered * inverse, inverse)


def time_embedding(steps):
    half_dim = FREQ // 2
    frequencies = jnp.exp(-math.log(10000.0) * jnp.arange(half_dim, dtype=jnp.float32) / half_dim)
    angles = steps.astype(jnp.float32)[:, None] * frequencies[None, :]
    return jnp.concatenate([jnp.cos(angles), jnp.sin(angles)], axis=1).astype(jnp.bfloat16)


def rotary_tables(positions):
    half_dim = HD // 2
    omegas = jnp.exp(-math.log(10000.0) * jnp.arange(half_dim, dtype=jnp.float32) / half_dim)
    angles = positions.astype(jnp.float32)[:, None] * omegas[None, :]
    return (jnp.cos(angles)[:, None, :], jnp.sin(angles)[:, None, :])


def rotate(values, cosine, sine_tab):
    half_dim = values.shape[-1] // 2
    first_half = values[..., :half_dim]
    second_half = values[..., half_dim:]
    return jnp.concatenate(
        [
            first_half * cosine - second_half * sine_tab,
            first_half * sine_tab + second_half * cosine,
        ],
        axis=-1,
    )


def unrotate(grads, cosine, sine_tab):
    half_dim = grads.shape[-1] // 2
    first_half = grads[..., :half_dim]
    second_half = grads[..., half_dim:]
    return jnp.concatenate(
        [
            first_half * cosine + second_half * sine_tab,
            second_half * cosine - first_half * sine_tab,
        ],
        axis=-1,
    )


def attend(query_rot, key_all, value_all, seq_len):
    query_count = query_rot.shape[0]
    block_len = min(query_count, 512)
    scale_dot = 1.0 / math.sqrt(HD)
    query_blocks = query_rot.reshape(query_count // block_len, block_len, query_rot.shape[1], HD)
    head_values = value_all.astype(jnp.float32)
    values_by_head = jnp.transpose(head_values)

    def block_step(state_in, query_block):
        d_keys, d_values, loss_sum = state_in
        scores = (
            jnp.einsum("qhd,khd->hqk", query_block, key_all, preferred_element_type=jnp.float32)
            * scale_dot
        )
        row_top = jnp.max(scores, axis=-1, keepdims=True)
        weights_exp = jnp.exp(scores - row_top)
        attn_probs = weights_exp / jnp.sum(weights_exp, axis=-1, keepdims=True)
        partial_value = jnp.einsum("hqk,kh->q", attn_probs, head_values, precision=exact_dots)
        logits = lax.psum(partial_value, "ctx")
        loss_sum = loss_sum + jnp.sum(jax.nn.softplus(-logits))
        d_logit = -jax.nn.sigmoid(-logits) / seq_len
        d_values = d_values + jnp.einsum("hqk,q->kh", attn_probs, d_logit, precision=exact_dots)
        d_probs = d_logit[None, :, None] * values_by_head[:, None, :]
        row_delta = jnp.sum(attn_probs * d_probs, axis=-1, keepdims=True)
        d_scores = (attn_probs * (d_probs - row_delta) * scale_dot).astype(jnp.bfloat16)
        d_query = jnp.einsum("hqk,khd->qhd", d_scores, key_all, preferred_element_type=jnp.float32)
        d_keys = d_keys + jnp.einsum(
            "hqk,qhd->khd", d_scores, query_block, preferred_element_type=jnp.float32
        )
        return ((d_keys, d_values, loss_sum), d_query)

    start_state = (
        jnp.zeros(key_all.shape, jnp.float32),
        jnp.zeros(head_values.shape, jnp.float32),
        jnp.zeros((), jnp.float32),
    )
    (d_keys, d_values, loss_sum), d_query = lax.scan(block_step, start_state, query_blocks)
    return (d_query.reshape(query_rot.shape), d_keys, d_values, loss_sum)


def fold_values(value_rows, disc_heads):
    head_count = disc_heads.shape[0]
    value_heads = value_rows.astype(jnp.float32).reshape(value_rows.shape[0], head_count, HD)
    return jnp.einsum("rhd,hd->rh", value_heads, disc_heads, precision=exact_dots)


def shards(latents, noise, steps, layout, w_time, w_student, w_qk, w_value, w_disc):
    clip_tokens = lax.all_gather(latents, "ctx", axis=0, tiled=True)
    block_len, channels = clip_tokens.shape
    col_count = w_student.shape[1]
    col_start = lax.axis_index("ctx") * col_count
    clip_index = lax.axis_index("dp")
    step_now = lax.dynamic_slice_in_dim(steps, clip_index, 1, 0)
    modulation = jnp.dot(time_embedding(step_now), w_time, preferred_element_type=jnp.float32)[0]
    shift_mod = modulation[:channels]
    scale_mod = modulation[channels : 2 * channels]
    gate_mod = modulation[2 * channels :]
    gate_cols = lax.dynamic_slice_in_dim(gate_mod, col_start, col_count, 0)
    sigma_clip = 0.25 + 0.5 * step_now.astype(jnp.float32)[0] / STEPS
    normed, unused_inverse = normalize(clip_tokens.astype(jnp.float32))
    mod_in = (normed * (1.0 + scale_mod) + shift_mod).astype(jnp.bfloat16)
    branch = jnp.dot(
        mod_in,
        lax.all_gather(w_student, "dp", axis=0, tiled=True),
        preferred_element_type=jnp.float32,
    )
    own_cols = lax.dynamic_slice_in_dim(clip_tokens, col_start, col_count, 1).astype(jnp.float32)
    student_cols = own_cols + gate_cols * branch
    teacher_part = (
        (1.0 - sigma_clip) * student_cols + sigma_clip * noise.astype(jnp.float32)
    ).astype(jnp.bfloat16)
    teacher_in = lax.all_gather(teacher_part, "ctx", axis=1, tiled=True)
    tnorm, inverse = normalize(teacher_in.astype(jnp.float32))
    tnorm_b = tnorm.astype(jnp.bfloat16)
    head_count = w_value.shape[1] // HD
    disc_heads = w_disc.reshape(head_count, HD)
    shard_fold = fold_values(w_value, disc_heads)
    qk_weights = lax.all_gather(w_qk, "dp", axis=0, tiled=True)
    folded = lax.all_gather(shard_fold, "dp", axis=0, tiled=True)
    qk_proj = jnp.dot(tnorm_b, qk_weights, preferred_element_type=jnp.float32).reshape(
        block_len, head_count, 2, HD
    )
    cosine, sine_tab = rotary_tables(layout[0])
    query_rot = rotate(qk_proj[:, :, 0], cosine, sine_tab).astype(jnp.bfloat16)
    key_rot = rotate(qk_proj[:, :, 1], cosine, sine_tab).astype(jnp.bfloat16)
    values_b = jnp.dot(
        tnorm_b, folded, precision=exact_dots, preferred_element_type=jnp.float32
    ).astype(jnp.bfloat16)
    d_query, d_keys, d_values, loss_sum = attend(query_rot, key_rot, values_b, block_len)
    d_key_own = lax.optimization_barrier(d_keys.astype(jnp.bfloat16)).astype(jnp.float32)
    d_values_own = lax.optimization_barrier(d_values.astype(jnp.bfloat16)).astype(jnp.float32)
    d_qk = jnp.stack(
        [unrotate(d_query, cosine, sine_tab), unrotate(d_key_own, cosine, sine_tab)], axis=2
    )
    d_qk = d_qk.reshape(block_len, head_count * 2 * HD).astype(jnp.bfloat16)
    d_part = lax.dot_general(
        d_qk, qk_weights, (((1,), (1,)), ((), ())), preferred_element_type=jnp.float32
    )
    d_part = d_part + lax.dot_general(
        d_values_own,
        folded,
        (((1,), (1,)), ((), ())),
        precision=exact_dots,
        preferred_element_type=jnp.float32,
    )
    d_tnorm = lax.psum(d_part, "ctx")
    d_in = inverse * (
        d_tnorm
        - jnp.mean(d_tnorm, axis=1, keepdims=True)
        - tnorm * jnp.mean(d_tnorm * tnorm, axis=1, keepdims=True)
    )
    d_cols = lax.dynamic_slice_in_dim(d_in, col_start, col_count, 1)
    d_branch = (gate_cols * (1.0 - sigma_clip) * d_cols).astype(jnp.bfloat16)
    student_grad = lax.psum_scatter(
        lax.dot_general(
            mod_in, d_branch, (((0,), (0,)), ((), ())), preferred_element_type=jnp.float32
        ),
        "dp",
        scatter_dimension=0,
        tiled=True,
    )
    clip_count = steps.shape[0]
    clip_ids = jnp.arange(clip_count, dtype=jnp.int32)
    loss_terms = jnp.where(clip_ids == clip_index, loss_sum / block_len, jnp.float32(0.0))
    clip_loss = lax.psum(loss_terms, "dp")
    return (clip_loss, student_grad)


def solution(mesh):
    return jax.shard_map(
        shards,
        mesh=mesh,
        in_specs=(
            P(("dp", "ctx"), None),
            P("dp", "ctx"),
            P(),
            P("dp", None),
            P(),
            P("dp", "ctx"),
            P("dp", "ctx"),
            P("dp", "ctx"),
            P("ctx"),
        ),
        out_specs=(P(), P("dp", "ctx")),
        check_vma=False,
    )
```

profile of v0, /device:TPU:8, one launch (start us, length us, event | category | flops | bytes accessed | tf_op | source)
XLA Modules:
  0.0 942.8 jit_solution(17932812151218208321)
XLA Ops:
  7.2 0.0 copy-start
  7.2 0.0 all-gather.6.cloned.1.call-start
  7.2 0.7 all-gather.6.cloned.1.call-update
  7.9 0.0 all-gather.8.cloned.1.call-start
  8.0 0.7 all-gather.8.cloned.1.call-update
  8.7 0.0 all-gather.10.cloned.1.call-start
  8.7 1.2 dynamic_slice.15
  10.6 0.1 sine_convert_fusion
  10.7 0.0 copy-start.16
  10.7 2.8 convolution_reduce_fusion
  13.5 0.1 broadcast_multiply_fusion
  13.6 34.7 %all-gather.6.cloned.1.call-done = bf16[512,2560]{1,0:T(8,128)(2,1)} async-done(((bf16[128,2560]{1,0:T(8,128)(2,1)}), bf16[512,2560]{1,0:T(8,128)(2,1)}) %all-gather.6.cloned.1.call-update) | async-done | bytes 2621456 | tf_op jit(solution)/shard_map/all_gather | solution.py:111
  48.3 2.3 convert_reduce_fusion.1
  50.7 0.2 copy-done.4
  50.9 0.8 fusion.6
  51.7 84.8 %all-gather.8.cloned.1.call-done = bf16[2560,640]{1,0:T(8,128)(2,1)} async-done(((bf16[40,640]{1,0:T(8,128)(2,1)}), bf16[2560,640]{1,0:T(8,128)(2,1)}) %all-gather.8.cloned.1.call-update) | async-done | bytes 3276816 | tf_op jit(solution)/shard_map/all_gather | solution.py:127
  136.5 5.4 fusion.33
  141.9 0.0 all-gather.10.cloned.1.call-update
  141.9 0.0 all-gather.12.cloned.1.call-start
  141.9 0.5 all-gather.12.cloned.1.call-update
  142.5 0.0 all-reduce.3.cloned.1.call-start
  142.6 0.2 fusion.53
  142.7 192.6 %all-gather = f32[64,40,5]{1,2,0:T(8,128)S(1)} all-gather(f32[1,40,5]{1,2,0:T(8,128)S(1)} %bitcast.67), channel_id=1, replica_groups=mesh['dp'=64,'ctx'=4] {'dp'}, dimensions={0}, use_global_device_ids=true | all-gather | bytes 52000 | tf_op jit(solution)/shard_map/all_gather | solution.py:142
  335.4 0.1 reshape.146
  335.5 1.8 multiply_cosine_fusion
  337.3 2.3 convert_reduce_fusion
  339.6 0.2 copy-done.3
  339.8 0.8 fusion.5
  340.7 2.4 fusion.43
  343.0 0.0 all-gather.12.cloned.1.call-done
  343.1 8.1 fusion.40
  351.1 4.6 reshape.142
  355.8 4.8 fusion.74
  360.6 0.1 copy.66
  360.7 0.1 copy.67
  360.8 0.7 copy-done.10
  361.5 0.1 copy-done.12
  361.6 0.9 subtract_convert_fusion.3
  362.5 1.3 multiply_reduce_fusion.1
  363.8 0.9 fusion.15
  364.7 0.9 fusion.14
  365.6 2.4 copy-done.2
  368.0 1.8 fusion.56
  369.8 5.9 psum.22
  375.7 0.6 negate_multiply_fusion
  376.3 7.4 fusion.42
  383.8 7.8 fusion.28
  391.6 6.9 fusion.76
  398.6 0.1 convert_element_type.97
  398.7 0.9 add_convert_fusion.1
  399.6 0.4 maximum_bitcast_fusion
  400.0 0.4 maximum_bitcast_fusion.1
  400.4 1.3 pad_maximum_fusion
  401.7 2.4 copy.37
  404.1 6.4 fusion.75
  410.5 4.8 convolution_add_fusion
  415.2 0.0 all-reduce.3.cloned.1.call-update
  415.3 0.0 reduce-scatter.5.cloned.1.call-start
  415.3 110.9 %all-reduce.3.cloned.1.call-done = f32[512,2560]{1,0:T(8,128)} async-done(((f32[512,2560]{1,0:T(8,128)}), f32[512,2560]{1,0:T(8,128)}) %all-reduce.3.cloned.1.call-update) | async-done | bytes 5242896 | tf_op jit(solution)/shard_map/psum | solution.py:169
  526.2 3.9 fusion.73
  530.1 6.9 fusion.46
  537.0 0.0 reduce-scatter.5.cloned.1.call-update
  537.7 188.7 %psum.23 = f32[64]{0:T(128)} all-reduce(f32[64]{0:T(128)S(1)} %compare_select_fusion.1), channel_id=1, replica_groups=mesh['dp'=64,'ctx'=4] {'dp'}, use_global_device_ids=true, to_apply=%region_8.9 | all-reduce | flops 64 | bytes 512 | tf_op jit(solution)/shard_map/psum | solution.py:188
  726.4 209.4 %reduce-scatter.5.cloned.1.call-done = f32[40,640]{1,0:T(8,128)} async-done(((f32[2560,640]{1,0:T(8,128)}), f32[40,640]{1,0:T(8,128)}) %reduce-scatter.5.cloned.1.call-update) | async-done | bytes 102416
  (46 shorter events, 0.2 us)
Async XLA Ops:
  7.2 135.4 %copy-start = (bf16[40,640]{1,0:T(8,128)(2,1)S(1)}, bf16[40,640]{1,0:T(8,128)(2,1)}, u32[]{:S(2)}) copy-start(bf16[40,640]{1,0:T(8,128)(2,1)} %param.16) | copy-start | bytes 153604
  7.2 41.2 %all-gather.6.cloned.1.call-start = ((), (), s32[]{:S(2)}) async-start(), calls=%async_computation.1 | async-start | bytes 3276800 | tf_op jit(solution)/shard_map/all_gather | solution.py:111
  7.9 128.5 %all-gather.8.cloned.1.call-start = ((), (), s32[]{:S(2)}) async-start(), calls=%async_computation.2 | async-start | bytes 3328000 | tf_op jit(solution)/shard_map/all_gather | solution.py:127
  8.7 328.7 %all-gather.10.cloned.1.call-start = ((), (), s32[]{:S(2)}) async-start(), calls=%async_computation.3 | async-start | bytes 3276800 | tf_op jit(solution)/shard_map/all_gather | solution.py:135
  10.7 125.7 %copy-start.16 = (bf16[512,640]{1,0:T(8,128)(2,1)S(1)}, bf16[512,640]{1,0:T(8,128)(2,1)}, u32[]{:S(2)}) copy-start(bf16[512,640]{1,0:T(8,128)(2,1)} %param.10) | copy-start | bytes 1966084
  48.3 2.5 copy-start.4
  136.5 6.1 copy-start.15
  136.5 6.1 copy-start.17
  141.9 201.2 %all-gather.12.cloned.1.call-start = ((), (), s32[]{:S(2)}) async-start(), calls=%async_computation.4 | async-start | bytes 6656000 | tf_op jit(solution)/shard_map/all_gather | solution.py:141
  142.5 383.7 %all-reduce.3.cloned.1.call-start = ((), (), s32[]{:S(2)}) async-start(), calls=%async_computation.5 | async-start | bytes 10485760 | tf_op jit(solution)/shard_map/psum | solution.py:169
  337.3 2.5 copy-start.3
  360.6 1.0 copy-start.10
  360.6 1.0 copy-start.12
  362.5 1.3 copy-start.7
  362.5 1.3 copy-start.8
  362.5 1.3 copy-start.9
  365.6 2.4 copy-start.2
  391.6 7.0 copy-start.14
  391.6 7.1 copy-start.6
  391.6 7.1 copy-start.11
  391.6 7.1 copy-start.13
  415.3 520.5 %reduce-scatter.5.cloned.1.call-start = ((), (), s32[]{:S(2)}) async-start(), calls=%async_computation.6 | async-start | bytes 6656000
  526.2 4.0 copy-start.5
  537.0 398.7 %copy-start.1 = (bf16[40,640]{1,0:T(8,128)(2,1)S(1)}, bf16[40,640]{1,0:T(8,128)(2,1)}, u32[]{:S(2)}) copy-start(bf16[40,640]{1,0:T(8,128)(2,1)} %param.16) | copy-start | bytes 153604
Sparse Core Ops, SparseCore 0:
  9.8 38.4 all-gather.5
  51.6 84.7 all-gather.7
  142.0 33.1 all-gather.9
  178.4 101.4 all-gather.11
  415.4 110.7 all-reduce.2
  537.2 398.5 reduce-scatter.4
where the time goes:
time: 956 us; the launch traced here: 943 us
  waiting for transfers between devices  442 us (46%)
  blocking collectives  387 us (40%)
  matrix products  62.1 us (6%)
  other arithmetic  18.5 us (2%)
  local copies, waits for them, and re-layouts  17.1 us (2%)
  between operations  16 us (2%)
    unnamed x7, waiting for transfers between devices  211 us
    all_gather x1, blocking collectives, shards(): folded = lax.all_gather(shard_fold, 'dp', axis=0, tiled=True)  193 us
    psum x1, blocking collectives, shards(): clip_loss = lax.psum(loss_terms, 'dp')  189 us
    psum x1, waiting for transfers between devices, shards(): d_tnorm = lax.psum(d_part, 'ctx')  111 us
    all_gather x1, waiting for transfers between devices, shards(): lax.all_gather(w_student, 'dp', axis=0, tiled=True)  84.8 us
    all_gather x1, waiting for transfers between devices, shards(): clip_tokens = lax.all_gather(latents, 'ctx', axis=0, tiled=True)  34.7 us
  transfers between devices with their start and end apart: 6, of which 4 were waited for; matrix products, arithmetic and copies ran while one was open for 2% of the time, Pallas kernels for 0%

commit v1 on v0

v1 whole, which is shorter than its diff:
```python
import functools
import math

import jax
import jax.numpy as jnp
from jax import lax
from jax.experimental import pallas as pl
from jax.experimental.pallas import tpu as pltpu
from jax.sharding import PartitionSpec as P

HD = 128
FREQ = 256
STEPS = 1000
MESH = pl.DeviceIdType.MESH
VMEM = pltpu.VMEM
VSPEC = pl.BlockSpec(memory_space=pltpu.VMEM)
ASPEC = pl.BlockSpec(memory_space=pl.ANY)
F32 = jnp.float32
BF16 = jnp.bfloat16


ln_eps = 1e-06
exact_dots = lax.Precision.HIGHEST


def place():
    d = lax.axis_index("dp")
    c = lax.axis_index("ctx")
    return d // 16, (d // 4) % 4, d % 4, c // 2, c % 2


class Links:
    def __init__(self, send_sems, recv_sems):
        self.send_sems, self.recv_sems = send_sems, recv_sems
        self.used = 0
        self.open = []
        self.zh, self.x, self.y, self.zl, self.core = place()

    def dev(self, zh=0, x=0, y=0, zl=0, core=0):
        z_new = (self.zh + zh) % 4
        x_new = (self.x + x) % 4
        y_new = (self.y + y) % 4
        return (
            z_new * 16 + x_new * 4 + y_new,
            ((self.zl + zl) % 2) * 2 + (self.core + core) % 2,
        )

    def barrier(self, steps):
        sem = pltpu.get_barrier_semaphore()
        for step in steps:
            pl.semaphore_signal(sem, inc=1, device_id=self.dev(**step), device_id_type=MESH)
        pl.semaphore_wait(sem, len(steps))

    def send(self, src, dst, **step):
        slot = self.used
        self.used += 1
        copy = pltpu.make_async_remote_copy(
            src_ref=src,
            dst_ref=dst,
            send_sem=self.send_sems.at[slot],
            recv_sem=self.recv_sems.at[slot],
            device_id=self.dev(**step),
            device_id_type=MESH,
        )
        copy.start()
        self.open.append(copy)
        return copy

    def drain(self):
        for copy in self.open:
            copy.wait_send()


def comm_call(body, outs, ins, sems, cid, scratch, in_specs, out_specs):
    return pl.pallas_call(
        body,
        out_shape=outs,
        in_specs=in_specs,
        out_specs=out_specs,
        scratch_shapes=[
            pltpu.SemaphoreType.DMA((sems,)),
            pltpu.SemaphoreType.DMA((sems,)),
            *scratch,
        ],
        compiler_params=pltpu.CompilerParams(
            collective_id=cid, has_side_effects=True, vmem_limit_bytes=56 << 20
        ),
    )(*ins)


AXES_AB = (("x", "y", 0), ("y", "x", 2))


def slot_of(links, axis, step, other=None, zs=slice(0, 2)):
    moved = {"x": links.x, "y": links.y}
    moved[axis] = (moved[axis] + step) % 4
    picks = dict(moved)
    if other is not None:
        picks[other] = slice(None)
    return (zs, picks["x"], picks["y"])


class Gather:
    def __init__(self, links, shard, out, loc_sem):
        self.links, self.shard, self.out = links, shard, out
        self.own = pltpu.make_async_copy(shard, out.at[links.zh, links.x, links.y], loc_sem)

    def along_z(self):
        links = self.links
        self.own.start()
        home = self.out.at[links.zh, links.x, links.y]
        self.copies = [links.send(self.shard, home, zh=step) for step in (1, 3, 2)]

    def settle(self):
        for copy in self.copies:
            copy.wait_recv()
        self.copies = []

    def spread(self, second):
        links = self.links
        if not second:
            self.own.wait()
        self.settle()
        self.near = []
        for first_axis, second_axis, base in AXES_AB:
            axis = second_axis if second else first_axis
            other = first_axis if second else None
            mine = self.out.at[slot_of(links, axis, 0, other, slice(base, base + 2))]
            self.near.append(
                (
                    axis,
                    other,
                    base,
                    links.send(mine, mine, **{axis: 1}),
                    links.send(mine, mine, **{axis: 3}),
                )
            )

    def relay(self):
        links = self.links
        self.copies = []
        for axis, other, base, up, down in self.near:
            up.wait_recv()
            piece = self.out.at[slot_of(links, axis, 3, other, base)]
            self.copies.append(links.send(piece, piece, **{axis: 1}))
            down.wait_recv()
            piece = self.out.at[slot_of(links, axis, 1, other, base + 1)]
            self.copies.append(links.send(piece, piece, **{axis: 3}))


NEAR = (
    dict(zh=1),
    dict(zh=2),
    dict(zh=3),
    dict(x=1),
    dict(x=3),
    dict(y=1),
    dict(y=3),
)


def gather_body(
    ws, wqk, fold, lat, ws_o, wqk_o, fold_o, lat_o, send_sems, recv_sems, loc_sems
):
    links = Links(send_sems, recv_sems)
    links.barrier(NEAR + (dict(core=1), dict(zl=1)))
    me = links.zl * 2 + links.core
    far = ((links.zl + 1) % 2) * 2 + links.core
    g_ws = Gather(links, ws, ws_o, loc_sems.at[0])
    g_fold = Gather(links, fold, fold_o, loc_sems.at[1])
    g_wqk = Gather(links, wqk, wqk_o, loc_sems.at[2])
    early = (g_ws, g_fold)
    for gather in early + (g_wqk,):
        gather.along_z()
    own = pltpu.make_async_copy(lat, lat_o.at[me], loc_sems.at[3])
    own.start()
    halves = [slice(0, 64), slice(64, 128)]
    across = [links.send(lat.at[h], lat_o.at[me, h], zl=1) for h in halves]
    beside = links.send(lat, lat_o.at[me], core=1)
    for gather in early + (g_wqk,):
        gather.spread(False)
    for gather in early:
        gather.relay()
    for gather in early:
        gather.spread(True)
    g_wqk.relay()
    for gather in early:
        gather.relay()
    g_wqk.spread(True)
    passed = []
    for copy, h in zip(across, halves):
        copy.wait_recv()
        passed.append(links.send(lat_o.at[far, h], lat_o.at[far, h], core=1))
    for gather in early:
        gather.settle()
    g_wqk.relay()
    own.wait()
    beside.wait_recv()
    for copy in passed:
        copy.wait_recv()
    g_wqk.settle()
    links.drain()


def gather_all(ws, wqk, fold, lat):
    outs = (
        jax.ShapeDtypeStruct((4, 4, 4) + ws.shape, ws.dtype),
        jax.ShapeDtypeStruct((4, 4, 4) + wqk.shape, wqk.dtype),
        jax.ShapeDtypeStruct((4, 4, 4) + fold.shape, fold.dtype),
        jax.ShapeDtypeStruct((4,) + lat.shape, lat.dtype),
    )
    return comm_call(
        gather_body,
        outs,
        (ws, wqk, fold, lat),
        64,
        1,
        [pltpu.SemaphoreType.DMA((4,))],
        [VSPEC] * 4,
        [ASPEC] * 4,
    )


CLIP_NEAR = (dict(core=1), dict(zl=1))
CLIP_ALL = CLIP_NEAR + (dict(zl=1, core=1),)


def teacher_body(part, full, send_sems, recv_sems, loc_sem):
    links = Links(send_sems, recv_sems)
    rows, cols = part.shape
    chunk = rows // 4

    def cut(owner, index):
        start = pl.multiple_of(owner * cols, 128)
        return full.at[pl.ds(index * chunk, chunk), pl.ds(start, cols)]

    me = links.zl * 2 + links.core
    far = ((links.zl + 1) % 2) * 2 + links.core
    links.barrier(CLIP_NEAR)
    own = pltpu.make_async_copy(part, full.at[:, pl.ds(pl.multiple_of(me * cols, 128), cols)], loc_sem)
    own.start()
    across, beside = [], []
    for index in range(4):
        piece = part.at[pl.ds(index * chunk, chunk)]
        across.append(links.send(piece, cut(me, index), zl=1))
        beside.append(links.send(piece, cut(me, index), core=1))
    passed = []
    for index, copy in enumerate(across):
        copy.wait_recv()
        passed.append(links.send(cut(far, index), cut(far, index), core=1))
    for copy in beside + passed:
        copy.wait_recv()
    own.wait()
    links.drain()


def teacher_gather(part):
    rows, cols = part.shape
    return comm_call(
        teacher_body,
        jax.ShapeDtypeStruct((rows, 4 * cols), part.dtype),
        (part,),
        12,
        2,
        [pltpu.SemaphoreType.DMA],
        [VSPEC],
        VSPEC,
    )


def reduce_clip_body(
    part, stats, out, stats_o, send_sems, recv_sems, stage, from_core, cross, from_chip, stats_in
):
    links = Links(send_sems, recv_sems)
    rows, cols = out.shape
    chunk = rows // 4
    core, zl = links.core, links.zl
    links.barrier(CLIP_ALL)
    tiny = [
        links.send(stats, stats_in.at[index], **step) for index, step in enumerate(CLIP_ALL)
    ]

    def block(z_to, core_to, index):
        start = pl.multiple_of((z_to * 2 + core_to) * cols, 128)
        return part[pl.ds(index * chunk, chunk), pl.ds(start, cols)]

    first = []
    for side in (1, 0):
        z_to = (zl + side) % 2
        for index in range(4):
            here = (side, pl.ds(index * chunk, chunk))
            stage[here] = block(z_to, (core + 1) % 2, index).astype(BF16)
            first.append(links.send(stage.at[here], from_core.at[here], core=1))
    second = []
    for index in range(4):
        here = (1, pl.ds(index * chunk, chunk))
        first[index].wait_recv()
        total = block((zl + 1) % 2, core, index) + from_core[here].astype(F32)
        rows_here = pl.ds(index * chunk, chunk)
        cross[rows_here] = total.astype(BF16)
        second.append(links.send(cross.at[rows_here], from_chip.at[rows_here], zl=1))
    for index in range(4):
        rows_here = pl.ds(index * chunk, chunk)
        first[4 + index].wait_recv()
        out[rows_here] = block(zl, core, index) + from_core[0, rows_here].astype(F32)
    for copy in tiny:
        copy.wait_recv()
    stats_o[...] = stats[...] + stats_in[0] + stats_in[1] + stats_in[2]
    for index in range(4):
        rows_here = pl.ds(index * chunk, chunk)
        second[index].wait_recv()
        out[rows_here] = out[rows_here] + from_chip[rows_here].astype(F32)
    links.drain()


def reduce_clip(part, stats):
    rows, cols = part.shape[0], part.shape[1] // 4
    return comm_call(
        reduce_clip_body,
        (
            jax.ShapeDtypeStruct((rows, cols), F32),
            jax.ShapeDtypeStruct(stats.shape, F32),
        ),
        (part, stats),
        15,
        3,
        [
            VMEM((2, rows, cols), BF16),
            VMEM((2, rows, cols), BF16),
            VMEM((rows, cols), BF16),
            VMEM((rows, cols), BF16),
            VMEM((3,) + stats.shape, F32),
        ],
        [VSPEC, VSPEC],
        (VSPEC, VSPEC),
    )


class Scatter:
    def __init__(self, links, axis, read, plain, bufs):
        self.links, self.axis, self.read, self.plain = links, axis, read, plain
        self.one_up, self.one_down, self.mix_up, self.mix_down, self.two_up, self.two_down = bufs

    def start(self):
        links, axis, plain = self.links, self.axis, self.plain
        self.up = links.send(plain(0, 2), self.one_up, **{axis: 1})
        self.down = links.send(plain(1, 2), self.one_down, **{axis: 3})
        self.last = [
            links.send(plain(1, 1), self.two_up.at[1], **{axis: 1}),
            links.send(plain(0, 3), self.two_down.at[0], **{axis: 3}),
        ]

    def middle(self):
        links, axis = self.links, self.axis
        self.up.wait_recv()
        self.mix_up[...] = (self.read(0, 1) + self.one_up[...].astype(F32)).astype(BF16)
        self.last.append(links.send(self.mix_up, self.two_up.at[0], **{axis: 1}))
        self.down.wait_recv()
        self.mix_down[...] = (self.read(1, 3) + self.one_down[...].astype(F32)).astype(BF16)
        self.last.append(links.send(self.mix_down, self.two_down.at[1], **{axis: 3}))

    def finish(self, store):
        for copy in self.last:
            copy.wait_recv()
        for half in range(2):
            store(
                half,
                self.read(half, 0)
                + self.two_up[half].astype(F32)
                + self.two_down[half].astype(F32),
            )


SCATTER_NEAR = NEAR + (dict(x=2), dict(y=2))


def scatter_body(part, loss, out, loss_o, send_sems, recv_sems, loss_buf, loss_mid, z_send, z_recv, z_keep, *bufs):
    links = Links(send_sems, recv_sems)
    links.barrier(SCATTER_NEAR)
    spare = list(bufs)
    stages = []
    for first_axis, second_axis, base in (("y", "x", 0), ("x", "y", 2)):
        big, spare = spare[:6], spare[6:]
        small, spare = spare[:6], spare[6:]
        mid, mid_b, spare = spare[0], spare[1], spare[2:]

        def plain1(half, step, axis=first_axis, other=second_axis, base=base):
            return part.at[slot_of(links, axis, step, other, base + half)]

        def read1(half, step, plain=plain1):
            return plain(half, step)[...].astype(F32)

        def spot(step, axis=second_axis):
            return ({"x": links.x, "y": links.y}[axis] + step) % 4

        def plain2(half, step, mid_b=mid_b, spot=spot):
            return mid_b.at[half, spot(step)]

        def read2(half, step, mid=mid, spot=spot):
            return mid[half, spot(step)]

        stages.append(
            (
                base,
                mid,
                mid_b,
                Scatter(links, first_axis, read1, plain1, big),
                Scatter(links, second_axis, read2, plain2, small),
            )
        )
    loss_mid[0] = loss[...]
    for stage in stages:
        stage[3].start()

    def loss_step(index, axis):
        return [
            links.send(loss_mid.at[index], loss_buf.at[index, step - 1], **{axis: step})
            for step in (1, 2, 3)
        ]

    def loss_sum(index, copies, store):
        for copy in copies:
            copy.wait_recv()
        store(loss_mid[index] + loss_buf[index, 0] + loss_buf[index, 1] + loss_buf[index, 2])

    def put_mid(index, value):
        loss_mid[index] = value

    tiny = loss_step(0, "y")
    for stage in stages:
        stage[3].middle()
    loss_sum(0, tiny, functools.partial(put_mid, 1))
    tiny = loss_step(1, "x")
    for base, mid, mid_b, first, second in stages:

        def store(half, value, mid=mid, mid_b=mid_b):
            mid[half] = value
            mid_b[half] = value.astype(BF16)

        first.finish(store)
        second.start()
    loss_sum(1, tiny, functools.partial(put_mid, 2))
    tiny = loss_step(2, "zh")
    for stage in stages:
        stage[4].middle()
    for base, mid, mid_b, first, second in stages:

        def keep(half, value, base=base):
            z_keep[base + half] = value
            z_send[base + half] = value.astype(BF16)

        second.finish(keep)
    tail = [
        links.send(z_send.at[(links.zh + step) % 4], z_recv.at[step - 1], zh=step)
        for step in (1, 3, 2)
    ]

    def put_loss(value):
        loss_o[...] = value

    loss_sum(2, tiny, put_loss)
    for copy in tail:
        copy.wait_recv()
    out[...] = (
        z_keep[links.zh]
        + z_recv[0].astype(F32)
        + z_recv[1].astype(F32)
        + z_recv[2].astype(F32)
    )
    links.drain()


def scatter_all(part, loss):
    rows, cols = part.shape[3:]
    big = [VMEM((4, rows, cols), BF16)] * 4 + [VMEM((2, 4, rows, cols), BF16)] * 2
    small = [VMEM((rows, cols), BF16)] * 4 + [VMEM((2, rows, cols), BF16)] * 2
    mids = [VMEM((2, 4, rows, cols), F32), VMEM((2, 4, rows, cols), BF16)]
    return comm_call(
        scatter_body,
        (
            jax.ShapeDtypeStruct((rows, cols), F32),
            jax.ShapeDtypeStruct(loss.shape, F32),
        ),
        (part, loss),
        40,
        4,
        [
            VMEM((3, 3) + loss.shape, F32),
            VMEM((3,) + loss.shape, F32),
            VMEM((4, rows, cols), BF16),
            VMEM((3, rows, cols), BF16),
            VMEM((4, rows, cols), F32),
        ]
        + (big + small + mids) * 2,
        [VSPEC, VSPEC],
        (VSPEC, VSPEC),
    )


def normalize(matrix):
    mean_row = jnp.mean(matrix, axis=-1, keepdims=True)
    centered = matrix - mean_row
    inverse = lax.rsqrt(jnp.mean(centered * centered, axis=-1, keepdims=True) + ln_eps)
    return (centered * inverse, inverse)


def time_embedding(steps):
    half_dim = FREQ // 2
    frequencies = jnp.exp(-math.log(10000.0) * jnp.arange(half_dim, dtype=jnp.float32) / half_dim)
    angles = steps.astype(jnp.float32)[:, None] * frequencies[None, :]
    return jnp.concatenate([jnp.cos(angles), jnp.sin(angles)], axis=1).astype(jnp.bfloat16)


def rotary_tables(positions):
    half_dim = HD // 2
    omegas = jnp.exp(-math.log(10000.0) * jnp.arange(half_dim, dtype=jnp.float32) / half_dim)
    angles = positions.astype(jnp.float32)[:, None] * omegas[None, :]
    return (jnp.cos(angles)[:, None, :], jnp.sin(angles)[:, None, :])


def rotate(values, cosine, sine_tab):
    half_dim = values.shape[-1] // 2
    first_half = values[..., :half_dim]
    second_half = values[..., half_dim:]
    return jnp.concatenate(
        [
            first_half * cosine - second_half * sine_tab,
            first_half * sine_tab + second_half * cosine,
        ],
        axis=-1,
    )


def unrotate(grads, cosine, sine_tab):
    half_dim = grads.shape[-1] // 2
    first_half = grads[..., :half_dim]
    second_half = grads[..., half_dim:]
    return jnp.concatenate(
        [
            first_half * cosine + second_half * sine_tab,
            second_half * cosine - first_half * sine_tab,
        ],
        axis=-1,
    )


def attend(query_block, key_all, value_all, seq_len):
    scale_dot = 1.0 / math.sqrt(HD)
    head_values = value_all.astype(jnp.float32)
    values_by_head = jnp.transpose(head_values)
    scores = (
        jnp.einsum("qhd,khd->hqk", query_block, key_all, preferred_element_type=jnp.float32)
        * scale_dot
    )
    row_top = jnp.max(scores, axis=-1, keepdims=True)
    weights_exp = jnp.exp(scores - row_top)
    attn_probs = weights_exp / jnp.sum(weights_exp, axis=-1, keepdims=True)
    partial_value = jnp.einsum("hqk,kh->q", attn_probs, head_values, precision=exact_dots)
    logits = lax.psum(partial_value, "ctx")
    loss_sum = jnp.sum(jax.nn.softplus(-logits))
    d_logit = -jax.nn.sigmoid(-logits) / seq_len
    d_values = jnp.einsum("hqk,q->kh", attn_probs, d_logit, precision=exact_dots)
    d_probs = d_logit[None, :, None] * values_by_head[:, None, :]
    row_delta = jnp.sum(attn_probs * d_probs, axis=-1, keepdims=True)
    d_scores = (attn_probs * (d_probs - row_delta) * scale_dot).astype(jnp.bfloat16)
    d_query = jnp.einsum("hqk,khd->qhd", d_scores, key_all, preferred_element_type=jnp.float32)
    d_keys = jnp.einsum("hqk,qhd->khd", d_scores, query_block, preferred_element_type=jnp.float32)
    return (d_query, d_keys, d_values, loss_sum)


def fold_values(value_rows, disc_heads):
    head_count = disc_heads.shape[0]
    value_heads = value_rows.astype(jnp.float32).reshape(value_rows.shape[0], head_count, HD)
    return jnp.einsum("rhd,hd->hr", value_heads, disc_heads, precision=exact_dots)


def shards(latents, noise, steps, layout, w_time, w_student, w_qk, w_value, w_disc):
    channels = latents.shape[1]
    block_len = noise.shape[0]
    rows_each, col_count = w_student.shape
    head_count = w_value.shape[1] // HD
    shard_fold = fold_values(w_value, w_disc.reshape(head_count, HD))
    fold_tile = jnp.pad(shard_fold, ((0, 8 - head_count), (0, 128 - rows_each)))
    ws_all, wqk_all, fold_all, lat_all = gather_all(w_student, w_qk, fold_tile, latents)
    student_weights = ws_all.reshape(channels, col_count)
    qk_weights = wqk_all.reshape(channels, w_qk.shape[1])
    folded = (
        fold_all[..., :head_count, :rows_each]
        .reshape(-1, head_count, rows_each)
        .transpose(0, 2, 1)
        .reshape(channels, head_count)
    )
    clip_tokens = lat_all.reshape(block_len, channels)
    col_start = lax.axis_index("ctx") * col_count
    clip_index = lax.axis_index("dp")
    step_now = lax.dynamic_slice_in_dim(steps, clip_index, 1, 0)
    modulation = jnp.dot(time_embedding(step_now), w_time, preferred_element_type=jnp.float32)[0]
    shift_mod = modulation[:channels]
    scale_mod = modulation[channels : 2 * channels]
    gate_mod = modulation[2 * channels :]
    gate_cols = lax.dynamic_slice_in_dim(gate_mod, col_start, col_count, 0)
    sigma_clip = 0.25 + 0.5 * step_now.astype(jnp.float32)[0] / STEPS
    normed, unused_inverse = normalize(clip_tokens.astype(jnp.float32))
    mod_in = (normed * (1.0 + scale_mod) + shift_mod).astype(jnp.bfloat16)
    branch = jnp.dot(mod_in, student_weights, preferred_element_type=jnp.float32)
    own_cols = lax.dynamic_slice_in_dim(clip_tokens, col_start, col_count, 1).astype(jnp.float32)
    student_cols = own_cols + gate_cols * branch
    teacher_part = (
        (1.0 - sigma_clip) * student_cols + sigma_clip * noise.astype(jnp.float32)
    ).astype(jnp.bfloat16)
    teacher_in = teacher_gather(teacher_part)
    tnorm, inverse = normalize(teacher_in.astype(jnp.float32))
    tnorm_b = tnorm.astype(jnp.bfloat16)
    qk_proj = jnp.dot(tnorm_b, qk_weights, preferred_element_type=jnp.float32).reshape(
        block_len, head_count, 2, HD
    )
    cosine, sine_tab = rotary_tables(layout[0])
    query_rot = rotate(qk_proj[:, :, 0], cosine, sine_tab).astype(jnp.bfloat16)
    key_rot = rotate(qk_proj[:, :, 1], cosine, sine_tab).astype(jnp.bfloat16)
    values_b = jnp.dot(
        tnorm_b, folded, precision=exact_dots, preferred_element_type=jnp.float32
    ).astype(jnp.bfloat16)
    d_query, d_keys, d_values, loss_sum = attend(query_rot, key_rot, values_b, block_len)
    d_key_own = lax.optimization_barrier(d_keys.astype(jnp.bfloat16)).astype(jnp.float32)
    d_values_own = lax.optimization_barrier(d_values.astype(jnp.bfloat16)).astype(jnp.float32)
    d_qk = jnp.stack(
        [unrotate(d_query, cosine, sine_tab), unrotate(d_key_own, cosine, sine_tab)], axis=2
    )
    d_qk = d_qk.reshape(block_len, head_count * 2 * HD).astype(jnp.bfloat16)
    d_part = lax.dot_general(
        d_qk, qk_weights, (((1,), (1,)), ((), ())), preferred_element_type=jnp.float32
    )
    d_part = d_part + lax.dot_general(
        d_values_own,
        folded,
        (((1,), (1,)), ((), ())),
        precision=exact_dots,
        preferred_element_type=jnp.float32,
    )
    sums = jnp.stack([jnp.sum(d_part, axis=1), jnp.sum(d_part * tnorm, axis=1)])
    d_tnorm, sums = reduce_clip(d_part, jnp.pad(sums, ((0, 6), (0, 0))))
    mean_d = (sums[0] / channels)[:, None]
    mean_dt = (sums[1] / channels)[:, None]
    tnorm_cols = lax.dynamic_slice_in_dim(tnorm, col_start, col_count, 1)
    d_cols = inverse * (d_tnorm - mean_d - tnorm_cols * mean_dt)
    d_branch = (gate_cols * (1.0 - sigma_clip) * d_cols).astype(jnp.bfloat16)
    grad_part = lax.dot_general(
        mod_in, d_branch, (((0,), (0,)), ((), ())), preferred_element_type=jnp.float32
    ).astype(jnp.bfloat16)
    lanes = lax.broadcasted_iota(jnp.int32, (8, 128), 1)
    loss_tile = jnp.where(lanes == clip_index, loss_sum / block_len, jnp.float32(0.0))
    student_grad, losses = scatter_all(
        grad_part.reshape(4, 4, 4, rows_each, col_count), loss_tile
    )
    clip_loss = losses[0, : steps.shape[0]]
    return (clip_loss, student_grad)


def solution(mesh):
    return jax.shard_map(
        shards,
        mesh=mesh,
        in_specs=(
            P(("dp", "ctx"), None),
            P("dp", "ctx"),
            P(),
            P("dp", None),
            P(),
            P("dp", "ctx"),
            P("dp", "ctx"),
            P("dp", "ctx"),
            P("ctx"),
        ),
        out_specs=(P(), P("dp", "ctx")),
        check_vma=False,
    )
```

time: 956 us -> 272 us (0.28); the launches traced: 943 us -> 271 us
  waiting for transfers between devices: 442 us -> 0 us
  blocking collectives: 387 us -> 7.79 us
  Pallas kernels: 0 us -> 157 us
  between operations: 16 us -> 2.38 us
    unnamed x7 -> x0, waiting for transfers between devices: 211 us -> none
    all_gather x1 -> x0, blocking collectives: 193 us -> none  [shards(): folded = lax.all_gather(shard_fold, 'dp', axis=0, tiled=True)]
    psum x2 -> x1, blocking collectives: 195 us -> 7.79 us  [attend(): logits = lax.psum(partial_value, 'ctx')]
    pallas_call x0 -> x4, Pallas kernels: none -> 157 us  [comm_call(): pl.pallas_call(body, out_shape=outs, in_specs=in_specs, out_specs=out_spe...]
    all_gather x4 -> x0, waiting for transfers between devices: 119 us -> none  [the longest x1 84.8 us: shards(): lax.all_gather(w_student, 'dp', axis=0, tiled=True)]
    psum x1 -> x0, waiting for transfers between devices: 111 us -> none  [shards(): d_tnorm = lax.psum(d_part, 'ctx')]
  transfers between devices with their start and end apart: 6 -> 0, of which waited for: 4 -> 0; matrix products, arithmetic and copies ran while one was open for 2% -> 0% of each run, Pallas kernels for 0% -> 0%
where the time goes in v1:
time: 272 us; the launch traced here: 271 us
  Pallas kernels  157 us (58%)
  matrix products  61.5 us (23%)
  other arithmetic  23.7 us (9%)
  local copies, waits for them, and re-layouts  18.9 us (7%)
  blocking collectives  7.79 us (3%)
    pallas_call x4, Pallas kernels, comm_call(): pl.pallas_call(body, out_shape=outs, in_specs=in_specs, out_specs=out_spe...  157 us
    dot_general x1, local copies, waits for them, and re-layouts, shards(): jnp.dot(tnorm_b, qk_weights, preferred_element_type=jnp.float32)  9.55 us
    psum x1, blocking collectives, attend(): logits = lax.psum(partial_value, 'ctx')  7.79 us
    dot_general x1, matrix products, shards(): lax.dot_general(d_values_own, folded, (((1,), (1,)), ((), ())), precision...  7.66 us
    dot_general x1, matrix products, attend(): jnp.einsum('hqk,khd->qhd', d_scores, key_all, preferred_element_type=jnp....  6.98 us
    dot_general x1, matrix products, attend(): jnp.einsum('hqk,qhd->khd', d_scores, query_block, preferred_element_type=...  6.95 us
    dot_general x1, matrix products, attend(): jnp.einsum('hqk,q->kh', attn_probs, d_logit, precision=exact_dots)  6.79 us
    dot_general x1, matrix products, shards(): lax.dot_general(mod_in, d_branch, (((0,), (0,)), ((), ())), preferred_ele...  6.36 us

profile of v1, /device:TPU:8, one launch (start us, length us, event | category | flops | bytes accessed | tf_op | source)
XLA Modules:
  0.0 271.0 jit_solution(1381945232543077843)
XLA Ops:
  0.6 0.0 copy-start
  0.7 1.2 dynamic_slice.12
  2.5 0.1 sine_convert_fusion
  2.6 2.7 %convolution_reduce_fusion = f32[7680]{0:T(1024)S(1)} fusion(bf16[256,1]{0,1:T(2,128)(2,1)S(1)} %reshape.216, bf16[256,7680]{1,0:T(8,128)(2,1)} %param.13), kind=kOutput, calls=%fused_computation.57 | convolution fusion | flops 3932160 | bytes 3963392 | tf_op jit(solution)/shard_map/dot_general | solution.py:597
  5.4 0.0 copy-start.10
  5.4 0.9 fusion.52
  6.3 0.6 pad.8.fold
  6.9 79.0 %shard_map.104 = (bf16[4,4,4,40,640]{4,3,2,1,0:T(8,128)(2,1)}, bf16[4,4,4,40,1280]{4,3,2,1,0:T(8,128)(2,1)}, f32[4,4,4,8,128]{4,3,2,1,0:T(8,128)}, bf16[4,128,2560]{2,1,0:T(8,128)(2,1)}) custom-call(bf16[40,640]{1,0:T(8,128)(2,1)} %ws.1, bf16[40,1280]{1,0:T(8,128)(2,1)} %wqk.1, f32[8,128]{1,0:T(8,128)} %pad.8.fold, bf16[128,2560]{1,0:T(8,128)(2,1)} %lat.1), custom_call_target="tpu_custom_call" | custom-call | tf_op jit(solution)/shard_map/pallas_call | solution.py:75
  85.9 0.0 copy-start.20
  85.9 2.3 convert_reduce_fusion.1
  88.2 0.6 fusion.68
  88.8 2.6 fusion.6
  91.4 0.6 add_rsqrt_fusion.1
  92.0 2.5 fusion.9
  94.5 0.7 broadcast_multiply_fusion
  95.2 5.8 %fusion.39.part = bf16[512,640]{1,0:T(8,128)(2,1)} fusion(bf16[512,2560]{1,0:T(8,128)(2,1)} %bitcast.92, bf16[2560,640]{1,0:T(8,128)(2,1)} %bitcast.106, bf16[512,640]{1,0:T(8,128)(2,1)S(1)} %copy-done.20, f32[]{:T(128)S(6)} %add_shard_map.3, f32[640]{0:T(1024)S(1)} %get-tuple-element.21, bf16[512,2560]{1,0:T(8,128)(2,1)S(1)} %bitcast.86, ...), kind=kOutput, calls=%fused_computation.48 | convolution fusion | flops 1680343040 | bytes 7866892 | tf_op jit(solution)/shard_map/dot_general | solution.py:605
  101.0 19.3 %shard_map.105 = bf16[512,2560]{1,0:T(8,128)(2,1)} custom-call(bf16[512,640]{1,0:T(8,128)(2,1)} %fusion.39.part), custom_call_target="tpu_custom_call" | custom-call | tf_op jit(solution)/shard_map/pallas_call | solution.py:75
  120.3 0.0 copy-start.3
  120.3 2.3 convert_reduce_fusion
  122.6 2.6 fusion.5
  125.2 0.0 copy-start.14
  125.2 0.0 copy-done.9
  125.2 0.1 reshape.212
  125.4 0.0 copy-done.3
  125.4 2.3 fusion.44
  127.7 9.5 %copy.17 = bf16[1280,2560]{1,0:T(8,128)(2,1)} copy(bf16[1280,2560]{0,1:T(8,128)(2,1)} %bitcast.88) | data formatting | bytes 13107200 | tf_op jit(solution)/shard_map/dot_general | solution.py:614
  137.3 0.0 copy-done.12
  137.3 6.1 %fusion.18 = f32[512,5,2,128]{0,3,2,1:T(8,128)S(1)} fusion(bf16[5,2,128,2560]{3,2,1,0:T(8,128)(2,1)} %bitcast.90, bf16[512,2560]{1,0:T(8,128)(2,1)S(1)} %copy-done.3, f32[512]{0:T(512)S(1)} %add_rsqrt_fusion, f32[512]{0:T(512)S(1)} %broadcast_multiply_fusion.1), kind=kOutput, calls=%fused_computation.30 | convolution fusion | flops 3360686080 | bytes 11800576 | tf_op jit(solution)/shard_map/dot_general | solution.py:614
  143.4 0.0 copy-start.19
  143.5 0.2 slice_bitcast_fusion.1
  143.7 0.4 copy-done.19
  144.1 0.5 multiply_cosine_fusion
  144.7 0.5 subtract_convert_fusion.3
  145.2 0.2 copy-done.8
  145.3 0.5 copy-done.6
  145.9 0.9 multiply_reduce_fusion.1
  146.8 0.9 fusion.15
  147.7 0.9 fusion.14
  148.6 2.4 copy-done.2
  151.0 1.8 fusion.55
  152.8 7.8 %psum.7 = f32[512]{0:T(512)S(1)} all-reduce(f32[512]{0:T(512)S(1)} %bitcast.103), channel_id=1, replica_groups=mesh['dp'=64,'ctx'=4] {'ctx'}, use_global_device_ids=true, to_apply=%region_6.7 | all-reduce | flops 512 | bytes 4096 | tf_op jit(solution)/shard_map/psum | solution.py:559
  160.6 0.6 fusion.59
  161.2 6.8 %fusion.75 = bf16[1,5,512]{2,0,1:T(2,128)(2,1)S(1)} fusion(f32[512,1,1]{0,1,2:T(1,128)S(1)} %bitcast.101, f32[5,512,512]{1,2,0:T(8,128)} %copy-done.2), kind=kOutput, calls=%fused_computation.122 | convolution fusion | flops 15728640 | bytes 5250048 | tf_op jit(solution)/shard_map/hqk,q->kh/dot_general | solution.py:562
  168.0 6.9 %fusion.43 = bf16[512,5,128]{0,2,1:T(8,128)(2,1)} fusion(f32[5,512,512]{1,2,0:T(8,128)} %copy-done.2, f32[5,512]{1,0:T(8,128)S(1)} %convert_bitcast_fusion, f32[512]{0:T(512)S(1)} %get-tuple-element.45, bf16[512,5,64]{0,2,1:T(8,128)(2,1)} %copy-done.6, bf16[512,5,64]{0,2,1:T(8,128)(2,1)} %copy-done.7), kind=kOutput, calls=%fused_computation.56 | convolution fusion | flops 346360832 | bytes 6565888 | tf_op jit(solution)/shard_map/hqk,qhd->khd/dot_general | solution.py:567
  175.0 2.4 convert_element_type.122
  177.3 7.0 %fusion.34 = f32[512,5,128]{0,2,1:T(8,128)} fusion(f32[5,512,512]{1,2,0:T(8,128)} %copy-done.2, f32[5,512]{1,0:T(8,128)S(1)} %convert_bitcast_fusion, f32[512]{0:T(512)S(1)} %get-tuple-element.45, bf16[512,5,64]{0,2,1:T(8,128)(2,1)S(1)} %get-tuple-element.30, bf16[512,5,64]{0,2,1:T(8,128)(2,1)S(1)} %get-tuple-element.29), kind=kOutput, calls=%fused_computation.43 | convolution fusion | flops 346033152 | bytes 7221248 | tf_op jit(solution)/shard_map/hqk,khd->qhd/dot_general | solution.py:566
  184.3 2.2 add_convert_fusion.3
  186.5 0.1 maximum_bitcast_fusion
  186.6 0.1 maximum_bitcast_fusion.1
  186.6 0.1 pad_maximum_fusion
  186.7 0.1 copy.24
  186.9 0.0 copy-start.15
  186.9 6.0 %fusion.74 = f32[512,2560]{1,0:T(8,128)S(1)} fusion(bf16[512,1280]{0,1:T(8,128)(2,1)S(1)} %bitcast.93, bf16[2560,1280]{1,0:T(8,128)(2,1)} %bitcast.89), kind=kOutput, calls=%fused_computation.121 | convolution fusion | flops 3355443200 | bytes 13107200 | tf_op jit(solution)/shard_map/dot_general | solution.py:630
  193.0 7.7 %fusion.72 = (f32[512]{0:T(512)S(1)}, f32[512]{0:T(512)S(1)}, f32[512,2560]{1,0:T(8,128)}, f32[512,2560]{1,0:T(8,128)}) fusion(f32[512]{0:T(512)S(1)} %copy-done.15, f32[512]{0:T(512)S(1)} %copy-done.13, bf16[512,2560]{1,0:T(8,128)(2,1)S(1)} %copy-done.3, f32[512,2560]{1,0:T(8,128)S(1)} %fusion.74, bf16[512,5]{0,1:T(8,128)(2,1)S(1)} %bitcast.97, ...), kind=kOutput, calls=%fused_computation.119 | convolution fusion | flops 87817216 | bytes 18414592 | tf_op jit(solution)/shard_map/dot_general | solution.py:633
  200.7 0.6 select_maximum_fusion.stats
  201.3 22.4 %shard_map.106 = (f32[512,640]{1,0:T(8,128)}, f32[8,512]{1,0:T(8,128)}) custom-call(f32[512,2560]{1,0:T(8,128)} %get-tuple-element.52.part, f32[8,512]{1,0:T(8,128)} %select_maximum_fusion.stats), custom_call_target="tpu_custom_call" | custom-call | tf_op jit(solution)/shard_map/pallas_call | solution.py:75
  223.7 0.8 slice_multiply_fusion.1
  224.5 0.0 copy-done.5
  224.6 0.0 copy-start.1
  224.6 6.4 %convolution_convert_fusion = bf16[2560,640]{1,0:T(8,128)(2,1)} fusion(bf16[512,2560]{1,0:T(8,128)(2,1)S(1)} %bitcast.87, f32[2560]{0:T(1024)S(1)} %get-tuple-element.38, f32[2560]{0:T(1024)S(1)} %copy-done.11, f32[512]{0:T(512)S(1)} %copy-done.18, f32[512]{0:T(512)S(1)} %copy-done.17, f32[512,2560]{1,0:T(8,128)} %get-tuple-element.22, s32[]{:T(128)S(6)} %select_n.17, ...), kind=kOutput, calls=%fused_computation.24 | convolution fusion | flops 1689190400 | bytes 8552964 | tf_op jit(solution)/shard_map/dot_general | solution.py:647
  231.6 0.6 iota.17.loss
  232.2 36.0 %shard_map.107 = (f32[40,640]{1,0:T(8,128)}, f32[8,128]{1,0:T(8,128)}) custom-call(bf16[4,4,4,40,640]{4,3,2,1,0:T(8,128)(2,1)} %bitcast.91, f32[8,128]{1,0:T(8,128)} %iota.17.loss), custom_call_target="tpu_custom_call" | custom-call | tf_op jit(solution)/shard_map/pallas_call | solution.py:75
  268.3 1.2 slice_bitcast_fusion.2
  269.4 1.5 copy.54
  (38 shorter events, 0.2 us)
Async XLA Ops:
  0.6 4.8 %copy-start = (bf16[40,640]{1,0:T(8,128)(2,1)S(1)}, bf16[40,640]{1,0:T(8,128)(2,1)}, u32[]{:S(2)}) copy-start(bf16[40,640]{1,0:T(8,128)(2,1)} %param.16) | copy-start | bytes 153604
  5.4 89.1 %copy-start.10 = (f32[2560]{0:T(1024)}, f32[2560]{0:T(1024)S(1)}, u32[]{:S(2)}) copy-start(f32[2560]{0:T(1024)S(1)} %get-tuple-element.39) | copy-start | bytes 30724
  85.9 6.1 %copy-start.4 = (bf16[4,128,2560]{2,1,0:T(8,128)(2,1)S(1)}, bf16[4,128,2560]{2,1,0:T(8,128)(2,1)}, u32[]{:S(2)}) copy-start(bf16[4,128,2560]{2,1,0:T(8,128)(2,1)} %get-tuple-element.10) | copy-start | bytes 7864324
  85.9 9.2 %copy-start.20 = (bf16[512,640]{1,0:T(8,128)(2,1)S(1)}, bf16[512,640]{1,0:T(8,128)(2,1)}, u32[]{:S(2)}) copy-start(bf16[512,640]{1,0:T(8,128)(2,1)} %param.10) | copy-start | bytes 1966084
  101.0 24.2 %copy-start.9 = (f32[4,4,4,8,128]{4,3,2,1,0:T(8,128)S(1)}, f32[4,4,4,8,128]{4,3,2,1,0:T(8,128)}, u32[]{:S(2)}) copy-start(f32[4,4,4,8,128]{4,3,2,1,0:T(8,128)} %get-tuple-element.13) | copy-start | bytes 786436
  120.3 5.1 %copy-start.3 = (bf16[512,2560]{1,0:T(8,128)(2,1)S(1)}, bf16[512,2560]{1,0:T(8,128)(2,1)}, u32[]{:S(2)}) copy-start(bf16[512,2560]{1,0:T(8,128)(2,1)} %shard_map.105) | copy-start | bytes 7864324
  122.6 14.7 %copy-start.12 = (f32[512]{0:T(512)}, f32[512]{0:T(512)S(1)}, u32[]{:S(2)}) copy-start(f32[512]{0:T(512)S(1)} %broadcast_multiply_fusion.1) | copy-start | bytes 6148
  125.2 12.1 %copy-start.14 = (f32[512]{0:T(512)}, f32[512]{0:T(512)S(1)}, u32[]{:S(2)}) copy-start(f32[512]{0:T(512)S(1)} %add_rsqrt_fusion) | copy-start | bytes 6148
  143.4 0.7 copy-start.19
  144.7 0.7 copy-start.8
  145.2 0.7 copy-start.6
  145.2 1.6 copy-start.7
  148.6 2.4 copy-start.2
  186.9 6.1 %copy-start.13 = (f32[512]{0:T(512)S(1)}, f32[512]{0:T(512)}, u32[]{:S(2)}) copy-start(f32[512]{0:T(512)} %copy-done.12) | copy-start | bytes 6148
  186.9 6.1 %copy-start.15 = (f32[512]{0:T(512)S(1)}, f32[512]{0:T(512)}, u32[]{:S(2)}) copy-start(f32[512]{0:T(512)} %copy-done.14) | copy-start | bytes 6148
  200.6 23.9 %copy-start.5 = (bf16[4,128,2560]{2,1,0:T(8,128)(2,1)S(1)}, bf16[4,128,2560]{2,1,0:T(8,128)(2,1)}, u32[]{:S(2)}) copy-start(bf16[4,128,2560]{2,1,0:T(8,128)(2,1)} %get-tuple-element.10) | copy-start | bytes 7864324
  200.6 23.9 %copy-start.11 = (f32[2560]{0:T(1024)S(1)}, f32[2560]{0:T(1024)}, u32[]{:S(2)}) copy-start(f32[2560]{0:T(1024)} %copy-done.10) | copy-start | bytes 30724
  200.6 23.9 %copy-start.16 = (f32[640]{0:T(1024)S(1)}, f32[640]{0:T(1024)}, u32[]{:S(2)}) copy-start(f32[640]{0:T(1024)} %get-tuple-element.20) | copy-start | bytes 7684
  200.6 23.9 %copy-start.17 = (f32[512]{0:T(512)S(1)}, f32[512]{0:T(512)}, u32[]{:S(2)}) copy-start(f32[512]{0:T(512)} %get-tuple-element.48) | copy-start | bytes 6148
  200.7 23.9 %copy-start.18 = (f32[512]{0:T(512)S(1)}, f32[512]{0:T(512)}, u32[]{:S(2)}) copy-start(f32[512]{0:T(512)} %get-tuple-element.47) | copy-start | bytes 6148
  224.6 46.4 %copy-start.1 = (bf16[40,640]{1,0:T(8,128)(2,1)S(1)}, bf16[40,640]{1,0:T(8,128)(2,1)}, u32[]{:S(2)}) copy-start(bf16[40,640]{1,0:T(8,128)(2,1)} %param.16) | copy-start | bytes 153604

commit v2 on v0

v2 whole, which is shorter than its diff:
```python
import functools
import math

import jax
import jax.numpy as jnp
from jax import lax
from jax.experimental import pallas as pl
from jax.experimental.pallas import tpu as pltpu
from jax.sharding import PartitionSpec as P

HD = 128
FREQ = 256
STEPS = 1000
MESH = pl.DeviceIdType.MESH
VMEM = pltpu.VMEM
VSPEC = pl.BlockSpec(memory_space=pltpu.VMEM)
ASPEC = pl.BlockSpec(memory_space=pl.ANY)
F32 = jnp.float32
BF16 = jnp.bfloat16


ln_eps = 1e-06
exact_dots = lax.Precision.HIGHEST


def place():
    d = lax.axis_index("dp")
    c = lax.axis_index("ctx")
    return d // 16, (d // 4) % 4, d % 4, c // 2, c % 2


class Links:
    def __init__(self, send_sems, recv_sems):
        self.send_sems, self.recv_sems = send_sems, recv_sems
        self.used = 0
        self.open = []
        self.zh, self.x, self.y, self.zl, self.core = place()

    def dev(self, zh=0, x=0, y=0, zl=0, core=0):
        z_new = (self.zh + zh) % 4
        x_new = (self.x + x) % 4
        y_new = (self.y + y) % 4
        return (
            z_new * 16 + x_new * 4 + y_new,
            ((self.zl + zl) % 2) * 2 + (self.core + core) % 2,
        )

    def barrier(self, steps):
        sem = pltpu.get_barrier_semaphore()
        for step in steps:
            pl.semaphore_signal(sem, inc=1, device_id=self.dev(**step), device_id_type=MESH)
        pl.semaphore_wait(sem, len(steps))

    def send(self, src, dst, **step):
        slot = self.used
        self.used += 1
        copy = pltpu.make_async_remote_copy(
            src_ref=src,
            dst_ref=dst,
            send_sem=self.send_sems.at[slot],
            recv_sem=self.recv_sems.at[slot],
            device_id=self.dev(**step),
            device_id_type=MESH,
        )
        copy.start()
        self.open.append(copy)
        return copy

    def drain(self):
        for copy in self.open:
            copy.wait_send()


AXES_AB = (("x", "y", 0), ("y", "x", 2))


def slot_of(links, axis, step, other=None, zs=slice(0, 2)):
    moved = {"x": links.x, "y": links.y}
    moved[axis] = (moved[axis] + step) % 4
    picks = dict(moved)
    if other is not None:
        picks[other] = slice(None)
    return (zs, picks["x"], picks["y"])


class Gather:
    def __init__(self, links, shard, out, loc_sem):
        self.links, self.shard, self.out = links, shard, out
        self.own = pltpu.make_async_copy(shard, out.at[links.zh, links.x, links.y], loc_sem)

    def along_z(self):
        links = self.links
        self.own.start()
        home = self.out.at[links.zh, links.x, links.y]
        self.copies = [links.send(self.shard, home, zh=step) for step in (1, 3, 2)]

    def settle(self):
        for copy in self.copies:
            copy.wait_recv()
        self.copies = []

    def spread(self, second):
        links = self.links
        if not second:
            self.own.wait()
        self.settle()
        self.near = []
        for first_axis, second_axis, base in AXES_AB:
            axis = second_axis if second else first_axis
            other = first_axis if second else None
            mine = self.out.at[slot_of(links, axis, 0, other, slice(base, base + 2))]
            self.near.append(
                (
                    axis,
                    other,
                    base,
                    links.send(mine, mine, **{axis: 1}),
                    links.send(mine, mine, **{axis: 3}),
                )
            )

    def relay(self):
        links = self.links
        self.copies = []
        for axis, other, base, up, down in self.near:
            up.wait_recv()
            piece = self.out.at[slot_of(links, axis, 3, other, base)]
            self.copies.append(links.send(piece, piece, **{axis: 1}))
            down.wait_recv()
            piece = self.out.at[slot_of(links, axis, 1, other, base + 1)]
            self.copies.append(links.send(piece, piece, **{axis: 3}))


NEAR = (
    dict(core=1),
    dict(zl=1),
    dict(zl=1, core=1),
    dict(zh=1),
    dict(zh=2),
    dict(zh=3),
    dict(x=1),
    dict(x=2),
    dict(x=3),
    dict(y=1),
    dict(y=2),
    dict(y=3),
)
CLIP_ALL = NEAR[:3]


class Scatter:
    def __init__(self, links, axis, read, plain, bufs):
        self.links, self.axis, self.read, self.plain = links, axis, read, plain
        self.one_up, self.one_down, self.mix_up, self.mix_down, self.two_up, self.two_down = bufs
        self.last = []

    def start(self, half):
        links, axis, plain = self.links, self.axis, self.plain
        if half == 0:
            self.up = links.send(plain(0, 2), self.one_up, **{axis: 1})
            self.last.append(links.send(plain(0, 3), self.two_down.at[0], **{axis: 3}))
        else:
            self.down = links.send(plain(1, 2), self.one_down, **{axis: 3})
            self.last.append(links.send(plain(1, 1), self.two_up.at[1], **{axis: 1}))

    def middle(self):
        links, axis = self.links, self.axis
        self.up.wait_recv()
        self.mix_up[...] = (self.read(0, 1) + self.one_up[...].astype(F32)).astype(BF16)
        self.last.append(links.send(self.mix_up, self.two_up.at[0], **{axis: 1}))
        self.down.wait_recv()
        self.mix_down[...] = (self.read(1, 3) + self.one_down[...].astype(F32)).astype(BF16)
        self.last.append(links.send(self.mix_down, self.two_down.at[1], **{axis: 3}))

    def finish(self, store):
        for copy in self.last:
            copy.wait_recv()
        for half in range(2):
            store(
                half,
                self.read(half, 0)
                + self.two_up[half].astype(F32)
                + self.two_down[half].astype(F32),
            )


def dot(a, b):
    return jnp.dot(a, b, preferred_element_type=F32)


def dot_t(a, b):
    return lax.dot_general(a, b, (((1,), (1,)), ((), ())), preferred_element_type=F32)


def lanes_of(row, count):
    return jnp.transpose(jnp.broadcast_to(row[0:1], (128, count)))


def step_body(
    lat, noise, steps, layout, w_time, ws, wqk, wv, disc,
    grad_o, loss_o,
    send_sems, recv_sems, loc_sems,
    wt, wx, ws_all, wx_all, lat_all, mod, modin, mod_t, part, tin, mean_c, inv_c,
    tables, qk, q_t, probs, pv, vrow, logit_s, logit_r, dlog, d_sc, dv_t, dqk,
    stage, from_core, cross, from_chip, own, sums, stats_s, stats_r, dbr,
    loss_buf, loss_mid, z_send, z_recv, z_keep, *bufs,
):
    links = Links(send_sems, recv_sems)
    tokens, cols = noise.shape
    channels = lat.shape[1]
    rows_each = lat.shape[0]
    heads = cols // HD
    dp, zl, core = lax.axis_index("dp"), links.zl, links.core
    me = zl * 2 + core
    beside_me = zl * 2 + (core + 1) % 2
    far = ((zl + 1) % 2) * 2 + core
    far_beside = ((zl + 1) % 2) * 2 + (core + 1) % 2
    fold_at = 2 * cols

    def col(owner, base=0):
        return pl.ds(pl.multiple_of(base + owner * cols, 128), cols)

    get_wt = pltpu.make_async_copy(w_time, wt, loc_sems.at[0])
    get_wt.start()
    links.barrier(NEAR)
    g_ws = Gather(links, ws, ws_all, loc_sems.at[1])
    g_wx = Gather(links, wx, wx_all, loc_sems.at[2])
    g_ws.along_z()

    lane = lax.broadcasted_iota(jnp.int32, (ws.shape[0], 128), 1)
    scaled = wv[...].astype(F32) * disc[...]
    extra = jnp.zeros((ws.shape[0], 128), F32)
    for head in range(heads):
        value = jnp.sum(scaled[:, head * HD : (head + 1) * HD], axis=1, keepdims=True)
        for term in range(3):
            piece = value.astype(BF16).astype(F32)
            extra = jnp.where(lane == term * 8 + head, piece, extra)
            value = value - piece
    wx[:, :fold_at] = wqk[...]
    wx[:, fold_at:] = extra.astype(BF16)
    g_wx.along_z()

    step_f = jnp.full((8, 128), steps[dp], jnp.int32).astype(F32)
    spot = lax.broadcasted_iota(jnp.int32, (8, 128), 1).astype(F32)
    angle = step_f * jnp.exp(-math.log(10000.0) * spot / (FREQ // 2))
    embed = jnp.concatenate([jnp.cos(angle), jnp.sin(angle)], axis=1).astype(BF16)
    sigma = (0.25 + 0.5 * step_f / STEPS)[0:1, 0:1]
    get_wt.wait()
    for third in range(3):
        here = slice(third * channels, (third + 1) * channels)
        mod[:, here] = dot(embed, wt[:, here])

    g_ws.spread(False)
    own_lat = pltpu.make_async_copy(lat, lat_all.at[me], loc_sems.at[3])
    own_lat.start()
    halves = [slice(0, rows_each // 2), slice(rows_each // 2, rows_each)]
    across = [links.send(lat.at[h], lat_all.at[me, h], zl=1) for h in halves]
    beside = links.send(lat, lat_all.at[me], core=1)

    def norm_rows(owner):
        def rows16(index, carry):
            rows = pl.ds(pl.multiple_of(index * 16, 16), 16)
            value = lat_all[owner, rows].astype(F32)
            value = value - jnp.sum(value, axis=1, keepdims=True) * (1.0 / channels)
            spread = jnp.sum(value * value, axis=1, keepdims=True) * (1.0 / channels)
            value = value * lax.rsqrt(spread + ln_eps)
            value = value * (1.0 + mod[0:1, channels : 2 * channels]) + mod[0:1, :channels]
            modin[pl.ds(pl.multiple_of(owner * rows_each + index * 16, 16), 16)] = value.astype(BF16)
            return carry

        lax.fori_loop(0, rows_each // 16, rows16, 0)

    own_lat.wait()
    norm_rows(me)
    g_ws.relay()
    g_ws.spread(True)
    g_wx.spread(False)
    beside.wait_recv()
    norm_rows(beside_me)
    g_ws.relay()
    g_wx.relay()
    g_wx.spread(True)
    passed = []
    for copy, h in zip(across, halves):
        copy.wait_recv()
        passed.append(links.send(lat_all.at[far, h], lat_all.at[far, h], core=1))
    norm_rows(far)
    for copy in passed:
        copy.wait_recv()
    norm_rows(far_beside)

    def flip(index, carry):
        here = pl.ds(pl.multiple_of(index * 128, 128), 128)
        mod_t[here] = jnp.transpose(modin[:, here].astype(F32)).astype(BF16)
        return carry

    g_ws.settle()
    gate = mod[0:1, col(me, 2 * channels)]
    keep = 1.0 - sigma
    size = tokens // 2
    sent, near = [], []
    for index in range(2):
        rows = pl.ds(index * size, size)
        branch = dot(modin[rows], ws_all[...].reshape(channels, cols))
        mine = lat_all[pl.ds(index * 2, 2), :, col(me)].reshape(size, cols).astype(F32)
        mixed = keep * (mine + gate * branch) + sigma * noise[rows].astype(F32)
        part[rows] = mixed.astype(BF16)
        sent.append(links.send(part.at[rows], tin.at[rows, col(me)], zl=1))
        near.append(links.send(part.at[rows], tin.at[rows, col(me)], core=1))
        tin[rows, col(me)] = mixed.astype(BF16)
    g_wx.relay()
    lax.fori_loop(0, channels // 128, flip, 0)

    place_c = lanes_of(layout[...].astype(F32), tokens)
    lane = lax.broadcasted_iota(jnp.int32, (tokens, 128), 1)
    omega = jnp.exp(-math.log(10000.0) * (lane % 64).astype(F32) / 64)
    tables[0] = jnp.cos(place_c * omega)
    sine = jnp.sin(place_c * omega)
    tables[1] = jnp.where(lane < 64, -sine, sine)

    passed = []
    for index in range(2):
        rows = pl.ds(index * size, size)
        sent[index].wait_recv()
        passed.append(links.send(tin.at[rows, col(far)], tin.at[rows, col(far)], core=1))
    tnorm_b = modin
    for index in range(2):
        near[index].wait_recv()
        passed[index].wait_recv()

        def rows16(step, carry):
            rows = pl.ds(pl.multiple_of(index * size + step * 16, 16), 16)
            value = tin[rows].astype(F32)
            mean = jnp.sum(value, axis=1, keepdims=True) * (1.0 / channels)
            value = value - mean
            spread = jnp.sum(value * value, axis=1, keepdims=True) * (1.0 / channels)
            inverse = lax.rsqrt(spread + ln_eps)
            tnorm_b[rows] = (value * inverse).astype(BF16)
            mean_c[rows] = jnp.broadcast_to(mean, (16, 128))
            inv_c[rows] = jnp.broadcast_to(inverse, (16, 128))
            return carry

        lax.fori_loop(0, size // 16, rows16, 0)
    g_wx.settle()
    links.drain()
    links.open = []

    def project(head, carry):
        weights = wx_all[:, :, :, :, pl.ds(pl.multiple_of(head * 256, 256), 256)]
        both = dot(tnorm_b[...], weights.reshape(channels, 256))
        cosine, sine = tables[0], tables[1]
        query, key = both[:, :HD], both[:, HD:]
        query = query * cosine + pltpu.roll(query, 64, 1) * sine
        key = key * cosine + pltpu.roll(key, 64, 1) * sine
        qk[:, pl.ds(pl.multiple_of(head * 256, 256), 128)] = query.astype(BF16)
        qk[:, pl.ds(pl.multiple_of(head * 256 + 128, 128), 128)] = key.astype(BF16)
        q_t[head] = jnp.transpose(query).astype(BF16)
        return carry

    lax.fori_loop(0, heads, project, 0)
    value_t = jnp.transpose(
        dot(tnorm_b[...], wx_all[:, :, :, :, pl.ds(fold_at, 128)].reshape(channels, 128))
    )
    vrow[...] = (value_t[0:8] + value_t[8:16] + value_t[16:24]).astype(BF16).astype(F32)

    scale_dot = 1.0 / math.sqrt(HD)
    block = 128
    blocks = tokens // block

    def attend(trip, carry):
        head, index = trip // blocks, trip % blocks
        rows = pl.ds(pl.multiple_of(index * block, block), block)
        query = qk[rows, pl.ds(pl.multiple_of(head * 256, 256), 128)]
        key = qk[:, pl.ds(pl.multiple_of(head * 256 + 128, 128), 128)]
        scores = dot_t(query, key) * scale_dot
        weights = jnp.exp(scores - jnp.max(scores, axis=1, keepdims=True))
        weights = weights * (1.0 / jnp.sum(weights, axis=1, keepdims=True))
        probs[head, rows] = weights
        share = jnp.sum(weights * vrow[pl.ds(head, 1)], axis=1, keepdims=True)
        pv[head, rows] = jnp.broadcast_to(share, (block, 128))
        return carry

    lax.fori_loop(0, heads * blocks, attend, 0)
    total = pv[0]
    for head in range(1, heads):
        total = total + pv[head]
    logit_s[...] = jnp.transpose(total)[0:8]
    tiny = [links.send(logit_s, logit_r.at[i], **step) for i, step in enumerate(CLIP_ALL)]
    dv_t[...] = jnp.zeros_like(dv_t)
    for copy in tiny:
        copy.wait_recv()
    logit = logit_s[...] + logit_r[0] + logit_r[1] + logit_r[2]
    soft = jnp.maximum(-logit, 0.0) + jnp.log1p(jnp.exp(-jnp.abs(logit)))
    loss = jnp.sum(soft, axis=1, keepdims=True) * (1.0 / tokens)
    lane = lax.broadcasted_iota(jnp.int32, (8, 128), 1)
    loss_mid[0] = jnp.where(lane == dp, jnp.broadcast_to(loss, (8, 128)), 0.0)

    def loss_step(index, axis):
        return [
            links.send(loss_mid.at[index], loss_buf.at[index, step - 1], **{axis: step})
            for step in (1, 2, 3)
        ]

    def loss_sum(index, copies):
        for copy in copies:
            copy.wait_recv()
        return loss_mid[index] + loss_buf[index, 0] + loss_buf[index, 1] + loss_buf[index, 2]

    tiny = loss_step(0, "y")
    dlog[...] = lanes_of((-1.0 / tokens) / (1.0 + jnp.exp(logit)), tokens)

    def backward(head, carry):
        def rows_of(index, d_value):
            rows = pl.ds(pl.multiple_of(index * block, block), block)
            weights = probs[head, rows]
            slope = dlog[rows][:, 0:1]
            tilt = vrow[pl.ds(head, 1)] - pv[head, rows][:, 0:1]
            d_sc[rows] = (weights * tilt * (slope * scale_dot)).astype(BF16)
            return d_value + jnp.sum(weights * slope, axis=0, keepdims=True)

        d_value = lax.fori_loop(0, blocks, rows_of, jnp.zeros((1, tokens), F32))
        d_value = d_value.astype(BF16).astype(F32)
        for term in range(3):
            dv_t[pl.ds(term * 8 + head, 1)] = d_value
        key = qk[:, pl.ds(pl.multiple_of(head * 256 + 128, 128), 128)]
        cosine, sine = tables[0], tables[1]
        d_query = dot(d_sc[...], key)
        d_key = jnp.transpose(dot(q_t[head], d_sc[...])).astype(BF16).astype(F32)
        d_query = d_query * cosine - pltpu.roll(d_query, 64, 1) * sine
        d_key = d_key * cosine - pltpu.roll(d_key, 64, 1) * sine
        dqk[:, pl.ds(pl.multiple_of(head * 256, 256), 128)] = d_query.astype(BF16)
        dqk[:, pl.ds(pl.multiple_of(head * 256 + 128, 128), 128)] = d_key.astype(BF16)
        return carry

    lax.fori_loop(0, heads, backward, 0)
    dqk[:, fold_at:] = jnp.transpose(dv_t[...]).astype(BF16)
    loss_mid[1] = loss_sum(0, tiny)
    tiny = loss_step(1, "x")

    sums[...] = jnp.zeros_like(sums)

    def d_block(owner, rows):
        weights = wx_all[owner].reshape(cols, wx.shape[1])
        value = dot_t(dqk[rows], weights)
        normed = (tin[rows, col(owner)].astype(F32) - mean_c[rows][:, 0:1]) * inv_c[rows][:, 0:1]
        sums[0, rows] = sums[0, rows] + jnp.sum(value, axis=1, keepdims=True)
        sums[1, rows] = sums[1, rows] + jnp.sum(value * normed, axis=1, keepdims=True)
        return value

    pieces = [pl.ds(index * size, size) for index in range(2)]
    first, second, third = [], [], []
    for rows in pieces:
        stage[1, rows] = d_block(far_beside, rows).astype(BF16)
        first.append(links.send(stage.at[1, rows], from_core.at[1, rows], core=1))
    for index, rows in enumerate(pieces):
        value = d_block(far, rows)
        first[index].wait_recv()
        cross[rows] = (value + from_core[1, rows].astype(F32)).astype(BF16)
        second.append(links.send(cross.at[rows], from_chip.at[rows], zl=1))
    for rows in pieces:
        stage[0, rows] = d_block(beside_me, rows).astype(BF16)
        third.append(links.send(stage.at[0, rows], from_core.at[0, rows], core=1))
    for rows in pieces:
        own[rows] = d_block(me, rows)
    loss_mid[2] = loss_sum(1, tiny)
    tiny = loss_step(2, "zh")
    stats_s[0:8] = jnp.transpose(sums[0])[0:8]
    stats_s[8:16] = jnp.transpose(sums[1])[0:8]
    stats = [links.send(stats_s, stats_r.at[i], **step) for i, step in enumerate(CLIP_ALL)]
    for copy in stats:
        copy.wait_recv()
    both = (stats_s[...] + stats_r[0] + stats_r[1] + stats_r[2]) * (1.0 / channels)
    sums[0] = lanes_of(both[0:8], tokens)
    sums[1] = lanes_of(both[8:16], tokens)
    for index, rows in enumerate(pieces):
        third[index].wait_recv()
        second[index].wait_recv()
        value = own[rows] + from_core[0, rows].astype(F32) + from_chip[rows].astype(F32)
        inverse = inv_c[rows][:, 0:1]
        normed = (tin[rows, col(me)].astype(F32) - mean_c[rows][:, 0:1]) * inverse
        value = inverse * (value - sums[0, rows][:, 0:1] - normed * sums[1, rows][:, 0:1])
        dbr[rows] = (gate * keep * value).astype(BF16)

    grads = ws_all
    spare = list(bufs)
    stages = []
    for first_axis, second_axis, base in (("y", "x", 0), ("x", "y", 2)):
        big, spare = spare[:6], spare[6:]
        small, spare = spare[:6], spare[6:]
        mid, mid_b, spare = spare[0], spare[1], spare[2:]

        def plain1(half, step, axis=first_axis, other=second_axis, base=base):
            return grads.at[slot_of(links, axis, step, other, base + half)]

        def read1(half, step, plain=plain1):
            return plain(half, step)[...].astype(F32)

        def spot_of(step, axis=second_axis):
            return ({"x": links.x, "y": links.y}[axis] + step) % 4

        def plain2(half, step, mid_b=mid_b, spot=spot_of):
            return mid_b.at[half, spot(step)]

        def read2(half, step, mid=mid, spot=spot_of):
            return mid[half, spot(step)]

        stages.append(
            (
                base,
                mid,
                mid_b,
                Scatter(links, first_axis, read1, plain1, big),
                Scatter(links, second_axis, read2, plain2, small),
            )
        )
    for quarter in (0, 2, 1, 3):
        here = pl.ds(quarter * cols, cols)
        value = dot(mod_t[here], dbr[...]).astype(BF16)
        grads[quarter] = value.reshape(grads.shape[1:])
        stages[quarter // 2][3].start(quarter % 2)
    for pair in stages:
        pair[3].middle()
    for base, mid, mid_b, first_ring, second_ring in stages:

        def store(half, value, mid=mid, mid_b=mid_b):
            mid[half] = value
            mid_b[half] = value.astype(BF16)

        first_ring.finish(store)
        second_ring.start(0)
        second_ring.start(1)
    for pair in stages:
        pair[4].middle()
    for base, mid, mid_b, first_ring, second_ring in stages:

        def hold(half, value, base=base):
            z_keep[base + half] = value
            z_send[base + half] = value.astype(BF16)

        second_ring.finish(hold)
    tail = [
        links.send(z_send.at[(links.zh + step) % 4], z_recv.at[step - 1], zh=step)
        for step in (1, 3, 2)
    ]
    loss_o[...] = loss_sum(2, tiny)
    for copy in tail:
        copy.wait_recv()
    grad_o[...] = (
        z_keep[links.zh]
        + z_recv[0].astype(F32)
        + z_recv[1].astype(F32)
        + z_recv[2].astype(F32)
    )
    links.drain()


def shards(latents, noise, steps, layout, w_time, w_student, w_qk, w_value, w_disc):
    channels = latents.shape[1]
    tokens, cols = noise.shape
    rows = w_student.shape[0]
    heads = cols // HD
    wide = w_qk.shape[1] + 128
    big = [VMEM((4, rows, cols), BF16)] * 4 + [VMEM((2, 4, rows, cols), BF16)] * 2
    small = [VMEM((rows, cols), BF16)] * 4 + [VMEM((2, rows, cols), BF16)] * 2
    mids = [VMEM((2, 4, rows, cols), F32), VMEM((2, 4, rows, cols), BF16)]
    scratch = [
        pltpu.SemaphoreType.DMA((128,)),
        pltpu.SemaphoreType.DMA((128,)),
        pltpu.SemaphoreType.DMA((4,)),
        VMEM(w_time.shape, BF16),
        VMEM((rows, wide), BF16),
        VMEM((4, 4, 4, rows, cols), BF16),
        VMEM((4, 4, 4, rows, wide), BF16),
        VMEM((4,) + latents.shape, BF16),
        VMEM((8, w_time.shape[1]), F32),
        VMEM((tokens, channels), BF16),
        VMEM((channels, tokens), BF16),
        VMEM((tokens, cols), BF16),
        VMEM((tokens, channels), BF16),
        VMEM((tokens, 128), F32),
        VMEM((tokens, 128), F32),
        VMEM((2, tokens, 128), F32),
        VMEM((tokens, 2 * cols), BF16),
        VMEM((heads, HD, tokens), BF16),
        VMEM((heads, tokens, tokens), F32),
        VMEM((heads, tokens, 128), F32),
        VMEM((8, tokens), F32),
        VMEM((8, tokens), F32),
        VMEM((3, 8, tokens), F32),
        VMEM((tokens, 128), F32),
        VMEM((tokens, tokens), BF16),
        VMEM((128, tokens), F32),
        VMEM((tokens, wide), BF16),
        VMEM((2, tokens, cols), BF16),
        VMEM((2, tokens, cols), BF16),
        VMEM((tokens, cols), BF16),
        VMEM((tokens, cols), BF16),
        VMEM((tokens, cols), F32),
        VMEM((2, tokens, 128), F32),
        VMEM((16, tokens), F32),
        VMEM((3, 16, tokens), F32),
        VMEM((tokens, cols), BF16),
        VMEM((3, 3, 8, 128), F32),
        VMEM((3, 8, 128), F32),
        VMEM((4, rows, cols), BF16),
        VMEM((3, rows, cols), BF16),
        VMEM((4, rows, cols), F32),
    ] + (big + small + mids) * 2
    student_grad, losses = pl.pallas_call(
        step_body,
        out_shape=(
            jax.ShapeDtypeStruct((rows, cols), F32),
            jax.ShapeDtypeStruct((8, 128), F32),
        ),
        in_specs=[
            VSPEC,
            VSPEC,
            pl.BlockSpec(memory_space=pltpu.SMEM),
            VSPEC,
            ASPEC,
            VSPEC,
            VSPEC,
            VSPEC,
            VSPEC,
        ],
        out_specs=(VSPEC, VSPEC),
        scratch_shapes=scratch,
        compiler_params=pltpu.CompilerParams(
            collective_id=1, has_side_effects=True, vmem_limit_bytes=67043328
        ),
    )(latents, noise, steps, layout, w_time, w_student, w_qk, w_value, w_disc.reshape(1, cols))
    return (losses[0, : steps.shape[0]], student_grad)


def solution(mesh):
    return jax.shard_map(
        shards,
        mesh=mesh,
        in_specs=(
            P(("dp", "ctx"), None),
            P("dp", "ctx"),
            P(),
            P("dp", None),
            P(),
            P("dp", "ctx"),
            P("dp", "ctx"),
            P("dp", "ctx"),
            P("ctx"),
        ),
        out_specs=(P(), P("dp", "ctx")),
        check_vma=False,
    )
```

time: 956 us -> 167 us (0.17); the launches traced: 943 us -> 166 us
  waiting for transfers between devices: 442 us -> 0 us
  blocking collectives: 387 us -> 0 us
  Pallas kernels: 0 us -> 161 us
  matrix products: 62.1 us -> 0 us
  other arithmetic: 18.5 us -> 0 us
  between operations: 16 us -> 0.64 us
  local copies, waits for them, and re-layouts: 17.1 us -> 3.99 us
    unnamed x7 -> x0, waiting for transfers between devices: 211 us -> none
    psum x2 -> x0, blocking collectives: 195 us -> none  [the longest x1 189 us: shards(): clip_loss = lax.psum(loss_terms, 'dp')]
    all_gather x1 -> x0, blocking collectives: 193 us -> none  [shards(): folded = lax.all_gather(shard_fold, 'dp', axis=0, tiled=True)]
    pallas_call x0 -> x1, Pallas kernels: none -> 161 us  [shards(): pl.pallas_call(step_body, out_shape=(jax.ShapeDtypeStruct((rows, cols), F...]
    all_gather x4 -> x0, waiting for transfers between devices: 119 us -> none  [the longest x1 84.8 us: shards(): lax.all_gather(w_student, 'dp', axis=0, tiled=True)]
    psum x1 -> x0, waiting for transfers between devices: 111 us -> none  [shards(): d_tnorm = lax.psum(d_part, 'ctx')]
    dot_general x13 -> x0, matrix products: 62.1 us -> none  [the longest x1 8.08 us: shards(): jnp.dot(tnorm_b, qk_weights, preferred_element_type=jnp.float32)]
    reduce_sum x6 -> x0, other arithmetic: 11.1 us -> none  [the longest x2 4.62 us: normalize(): mean_row = jnp.mean(matrix, axis=-1, keepdims=True)]
  transfers between devices with their start and end apart: 6 -> 0, of which waited for: 4 -> 0; matrix products, arithmetic and copies ran while one was open for 2% -> 0% of each run, Pallas kernels for 0% -> 0%
where the time goes in v2:
time: 167 us; the launch traced here: 166 us
  Pallas kernels  161 us (96%)
  local copies, waits for them, and re-layouts  3.99 us (2%)
    pallas_call x1, Pallas kernels, shards(): pl.pallas_call(step_body, out_shape=(jax.ShapeDtypeStruct((rows, cols), F...  161 us

profile of v2, /device:TPU:8, one launch (start us, length us, event | category | flops | bytes accessed | tf_op | source)
XLA Modules:
  0.0 165.5 jit_solution(4816777301107766351)
XLA Ops:
  0.6 1.3 reshape.7.disc
  1.9 160.9 %shard_map.104 = (f32[40,640]{1,0:T(8,128)}, f32[8,128]{1,0:T(8,128)}) custom-call(bf16[128,2560]{1,0:T(8,128)(2,1)} %lat.1, bf16[512,640]{1,0:T(8,128)(2,1)} %noise.1, s32[64]{0:T(128)} %steps.1, s32[1,512]{1,0:T(1,128)} %layout.1, bf16[256,7680]{1,0:T(8,128)(2,1)} %w_time.1, bf16[40,640]{1,0:T(8,128)(2,1)} %ws.1, bf16[40,1280]{1,0:T(8,128)(2,1)} %wqk.1, ...), custom_call_target="tpu_custom_call" | custom-call | tf_op jit(solution)/shard_map/pallas_call | solution.py:609
  162.8 1.2 slice_bitcast_fusion
  164.0 1.5 copy.12

commit v3 on v2

--- a/solution.py
+++ b/solution.py
@@ -200,7 +200,7 @@
     lat, noise, steps, layout, w_time, ws, wqk, wv, disc,
     grad_o, loss_o,
     send_sems, recv_sems, loc_sems,
-    wt, wx, ws_all, wx_all, lat_all, mod, modin, mod_t, part, tin, mean_c, inv_c,
+    wt, wx_1, wx_2, ws_all, wx_1_all, wx_2_all, lat_all, mod, modin, mod_t, part, tin, mean_c, inv_c,
     tables, qk, q_t, probs, pv, vrow, logit_s, logit_r, dlog, d_sc, dv_t, dqk,
     stage, from_core, cross, from_chip, own, sums, stats_s, stats_r, dbr,
     loss_buf, loss_mid, z_send, z_recv, z_keep, *bufs,
@@ -215,7 +215,9 @@
     beside_me = zl * 2 + (core + 1) % 2
     far = ((zl + 1) % 2) * 2 + core
     far_beside = ((zl + 1) % 2) * 2 + (core + 1) % 2
-    fold_at = 2 * cols
+    early = (heads - 1) // 2
+    fold_at = early * 2 * HD
+    late_at = fold_at + 128
 
     def col(owner, base=0):
         return pl.ds(pl.multiple_of(base + owner * cols, 128), cols)
@@ -224,7 +226,8 @@
     get_wt.start()
     links.barrier(NEAR)
     g_ws = Gather(links, ws, ws_all, loc_sems.at[1])
-    g_wx = Gather(links, wx, wx_all, loc_sems.at[2])
+    g_1 = Gather(links, wx_1, wx_1_all, loc_sems.at[2])
+    g_2 = Gather(links, wx_2, wx_2_all, loc_sems.at[4])
     g_ws.along_z()
 
     lane = lax.broadcasted_iota(jnp.int32, (ws.shape[0], 128), 1)
@@ -236,20 +239,16 @@
             piece = value.astype(BF16).astype(F32)
             extra = jnp.where(lane == term * 8 + head, piece, extra)
             value = value - piece
-    wx[:, :fold_at] = wqk[...]
-    wx[:, fold_at:] = extra.astype(BF16)
-    g_wx.along_z()
+    wx_1[:, :fold_at] = wqk[:, :fold_at]
+    wx_1[:, fold_at:] = extra.astype(BF16)
+    wx_2[...] = wqk[:, fold_at:]
+    g_1.along_z()
 
     step_f = jnp.full((8, 128), steps[dp], jnp.int32).astype(F32)
     spot = lax.broadcasted_iota(jnp.int32, (8, 128), 1).astype(F32)
     angle = step_f * jnp.exp(-math.log(10000.0) * spot / (FREQ // 2))
     embed = jnp.concatenate([jnp.cos(angle), jnp.sin(angle)], axis=1).astype(BF16)
     sigma = (0.25 + 0.5 * step_f / STEPS)[0:1, 0:1]
-    get_wt.wait()
-    for third in range(3):
-        here = slice(third * channels, (third + 1) * channels)
-        mod[:, here] = dot(embed, wt[:, here])
-
     g_ws.spread(False)
     own_lat = pltpu.make_async_copy(lat, lat_all.at[me], loc_sems.at[3])
     own_lat.start()
@@ -271,20 +270,26 @@
         lax.fori_loop(0, rows_each // 16, rows16, 0)
 
     own_lat.wait()
-    norm_rows(me)
+    get_wt.wait()
+    for third in range(3):
+        here = slice(third * channels, (third + 1) * channels)
+        mod[:, here] = dot(embed, wt[:, here])
     g_ws.relay()
     g_ws.spread(True)
-    g_wx.spread(False)
+    g_1.spread(False)
+    g_2.along_z()
+    norm_rows(me)
     beside.wait_recv()
     norm_rows(beside_me)
     g_ws.relay()
-    g_wx.relay()
-    g_wx.spread(True)
+    g_1.relay()
+    g_1.spread(True)
     passed = []
     for copy, h in zip(across, halves):
         copy.wait_recv()
         passed.append(links.send(lat_all.at[far, h], lat_all.at[far, h], core=1))
     norm_rows(far)
+    g_2.spread(False)
     for copy in passed:
         copy.wait_recv()
     norm_rows(far_beside)
@@ -308,7 +313,9 @@
         sent.append(links.send(part.at[rows], tin.at[rows, col(me)], zl=1))
         near.append(links.send(part.at[rows], tin.at[rows, col(me)], core=1))
         tin[rows, col(me)] = mixed.astype(BF16)
-    g_wx.relay()
+    g_1.relay()
+    g_2.relay()
+    g_2.spread(True)
     lax.fori_loop(0, channels // 128, flip, 0)
 
     place_c = lanes_of(layout[...].astype(F32), tokens)
@@ -341,12 +348,10 @@
             return carry
 
         lax.fori_loop(0, size // 16, rows16, 0)
-    g_wx.settle()
-    links.drain()
-    links.open = []
-
-    def project(head, carry):
-        weights = wx_all[:, :, :, :, pl.ds(pl.multiple_of(head * 256, 256), 256)]
+    g_1.settle()
+
+    def project(head, source, base):
+        weights = source[:, :, :, :, pl.ds(pl.multiple_of(head * 256 - base, 256), 256)]
         both = dot(tnorm_b[...], weights.reshape(channels, 256))
         cosine, sine = tables[0], tables[1]
         query, key = both[:, :HD], both[:, HD:]
@@ -355,13 +360,6 @@
         qk[:, pl.ds(pl.multiple_of(head * 256, 256), 128)] = query.astype(BF16)
         qk[:, pl.ds(pl.multiple_of(head * 256 + 128, 128), 128)] = key.astype(BF16)
         q_t[head] = jnp.transpose(query).astype(BF16)
-        return carry
-
-    lax.fori_loop(0, heads, project, 0)
-    value_t = jnp.transpose(
-        dot(tnorm_b[...], wx_all[:, :, :, :, pl.ds(fold_at, 128)].reshape(channels, 128))
-    )
-    vrow[...] = (value_t[0:8] + value_t[8:16] + value_t[16:24]).astype(BF16).astype(F32)
 
     scale_dot = 1.0 / math.sqrt(HD)
     block = 128
@@ -380,7 +378,26 @@
         pv[head, rows] = jnp.broadcast_to(share, (block, 128))
         return carry
 
-    lax.fori_loop(0, heads * blocks, attend, 0)
+    def project_early(head, carry):
+        project(head, wx_1_all, 0)
+        return carry
+
+    def project_late(head, carry):
+        project(head, wx_2_all, fold_at)
+        return carry
+
+    lax.fori_loop(0, early, project_early, 0)
+    value_t = jnp.transpose(
+        dot(tnorm_b[...], wx_1_all[:, :, :, :, pl.ds(fold_at, 128)].reshape(channels, 128))
+    )
+    vrow[...] = (value_t[0:8] + value_t[8:16] + value_t[16:24]).astype(BF16).astype(F32)
+    g_2.relay()
+    lax.fori_loop(0, early * blocks, attend, 0)
+    g_2.settle()
+    links.drain()
+    links.open = []
+    lax.fori_loop(early, heads, project_late, 0)
+    lax.fori_loop(early * blocks, heads * blocks, attend, 0)
     total = pv[0]
     for head in range(1, heads):
         total = total + pv[head]
@@ -428,20 +445,21 @@
         d_key = jnp.transpose(dot(q_t[head], d_sc[...])).astype(BF16).astype(F32)
         d_query = d_query * cosine - pltpu.roll(d_query, 64, 1) * sine
         d_key = d_key * cosine - pltpu.roll(d_key, 64, 1) * sine
-        dqk[:, pl.ds(pl.multiple_of(head * 256, 256), 128)] = d_query.astype(BF16)
-        dqk[:, pl.ds(pl.multiple_of(head * 256 + 128, 128), 128)] = d_key.astype(BF16)
+        start = head * 256 + ((head + early) // (2 * early)) * 128
+        dqk[:, pl.ds(pl.multiple_of(start, 128), 128)] = d_query.astype(BF16)
+        dqk[:, pl.ds(pl.multiple_of(start + 128, 128), 128)] = d_key.astype(BF16)
         return carry
 
     lax.fori_loop(0, heads, backward, 0)
-    dqk[:, fold_at:] = jnp.transpose(dv_t[...]).astype(BF16)
+    dqk[:, fold_at:late_at] = jnp.transpose(dv_t[...]).astype(BF16)
     loss_mid[1] = loss_sum(0, tiny)
     tiny = loss_step(1, "x")
 
     sums[...] = jnp.zeros_like(sums)
 
     def d_block(owner, rows):
-        weights = wx_all[owner].reshape(cols, wx.shape[1])
-        value = dot_t(dqk[rows], weights)
+        value = dot_t(dqk[rows, :late_at], wx_1_all[owner].reshape(cols, late_at))
+        value = value + dot_t(dqk[rows, late_at:], wx_2_all[owner].reshape(cols, -1))
         normed = (tin[rows, col(owner)].astype(F32) - mean_c[rows][:, 0:1]) * inv_c[rows][:, 0:1]
         sums[0, rows] = sums[0, rows] + jnp.sum(value, axis=1, keepdims=True)
         sums[1, rows] = sums[1, rows] + jnp.sum(value * normed, axis=1, keepdims=True)
@@ -560,17 +578,20 @@
     rows = w_student.shape[0]
     heads = cols // HD
     wide = w_qk.shape[1] + 128
+    narrow = (heads - 1) // 2 * 2 * HD + 128
     big = [VMEM((4, rows, cols), BF16)] * 4 + [VMEM((2, 4, rows, cols), BF16)] * 2
     small = [VMEM((rows, cols), BF16)] * 4 + [VMEM((2, rows, cols), BF16)] * 2
     mids = [VMEM((2, 4, rows, cols), F32), VMEM((2, 4, rows, cols), BF16)]
     scratch = [
         pltpu.SemaphoreType.DMA((128,)),
         pltpu.SemaphoreType.DMA((128,)),
-        pltpu.SemaphoreType.DMA((4,)),
+        pltpu.SemaphoreType.DMA((5,)),
         VMEM(w_time.shape, BF16),
-        VMEM((rows, wide), BF16),
+        VMEM((rows, narrow), BF16),
+        VMEM((rows, wide - narrow), BF16),
         VMEM((4, 4, 4, rows, cols), BF16),
-        VMEM((4, 4, 4, rows, wide), BF16),
+        VMEM((4, 4, 4, rows, narrow), BF16),
+        VMEM((4, 4, 4, rows, wide - narrow), BF16),
         VMEM((4,) + latents.shape, BF16),
         VMEM((8, w_time.shape[1]), F32),
         VMEM((tokens, channels), BF16),

time: 167 us -> 166 us (level)
  no operation moved by 1% of the time
where the time goes in v3:
time: 166 us
  Pallas kernels  161 us (97%)
  local copies, waits for them, and re-layouts  3.99 us (2%)
    pallas_call x1, Pallas kernels, shards(): pl.pallas_call(step_body, out_shape=(jax.ShapeDtypeStruct((rows, cols), F...  161 us

profile of v3, /device:TPU:8, one launch (start us, length us, event | category | flops | bytes accessed | tf_op | source)
XLA Modules:
  0.0 165.9 jit_solution(16320579813783237909)
XLA Ops:
  0.6 1.3 reshape.7.disc
  1.9 161.3 %shard_map.104 = (f32[40,640]{1,0:T(8,128)}, f32[8,128]{1,0:T(8,128)}) custom-call(bf16[128,2560]{1,0:T(8,128)(2,1)} %lat.1, bf16[512,640]{1,0:T(8,128)(2,1)} %noise.1, s32[64]{0:T(128)} %steps.1, s32[1,512]{1,0:T(1,128)} %layout.1, bf16[256,7680]{1,0:T(8,128)(2,1)} %w_time.1, bf16[40,640]{1,0:T(8,128)(2,1)} %ws.1, bf16[40,1280]{1,0:T(8,128)(2,1)} %wqk.1, ...), custom_call_target="tpu_custom_call" | custom-call | tf_op jit(solution)/shard_map/pallas_call | solution.py:630
  163.2 1.2 slice_bitcast_fusion
  164.4 1.5 copy.12

commit v4 on v3

--- a/solution.py
+++ b/solution.py
@@ -182,6 +182,26 @@
                 + self.two_up[half].astype(F32)
                 + self.two_down[half].astype(F32),
             )
+
+
+class Direct:
+    def __init__(self, links, axis, read, plain, inbox):
+        self.links, self.axis, self.read, self.plain, self.inbox = links, axis, read, plain, inbox
+
+    def start(self):
+        self.copies = [
+            self.links.send(self.plain(step), self.inbox.at[step - 1], **{self.axis: step})
+            for step in (1, 3, 2)
+        ]
+
+    def finish(self, store):
+        for copy in self.copies:
+            copy.wait_recv()
+        for half in range(2):
+            value = self.read(half)
+            for index in range(3):
+                value = value + self.inbox[index, half].astype(F32)
+            store(half, value)
 
 
 def dot(a, b):
@@ -231,7 +251,7 @@
     g_ws.along_z()
 
     lane = lax.broadcasted_iota(jnp.int32, (ws.shape[0], 128), 1)
-    scaled = wv[...].astype(F32) * disc[...]
+    scaled = wv[...].astype(F32) * disc[...].reshape(1, cols)
     extra = jnp.zeros((ws.shape[0], 128), F32)
     for head in range(heads):
         value = jnp.sum(scaled[:, head * HD : (head + 1) * HD], axis=1, keepdims=True)
@@ -243,18 +263,23 @@
     wx_1[:, fold_at:] = extra.astype(BF16)
     wx_2[...] = wqk[:, fold_at:]
     g_1.along_z()
+    own_lat = pltpu.make_async_copy(lat, lat_all.at[me], loc_sems.at[3])
+    own_lat.start()
+    halves = [slice(0, rows_each // 2), slice(rows_each // 2, rows_each)]
+    across = [links.send(lat.at[h], lat_all.at[me, h], zl=1) for h in halves]
+    beside = links.send(lat, lat_all.at[me], core=1)
+    g_2.along_z()
 
     step_f = jnp.full((8, 128), steps[dp], jnp.int32).astype(F32)
     spot = lax.broadcasted_iota(jnp.int32, (8, 128), 1).astype(F32)
     angle = step_f * jnp.exp(-math.log(10000.0) * spot / (FREQ // 2))
     embed = jnp.concatenate([jnp.cos(angle), jnp.sin(angle)], axis=1).astype(BF16)
     sigma = (0.25 + 0.5 * step_f / STEPS)[0:1, 0:1]
+    get_wt.wait()
+    for third in range(3):
+        here = slice(third * channels, (third + 1) * channels)
+        mod[:, here] = dot(embed, wt[:, here])
     g_ws.spread(False)
-    own_lat = pltpu.make_async_copy(lat, lat_all.at[me], loc_sems.at[3])
-    own_lat.start()
-    halves = [slice(0, rows_each // 2), slice(rows_each // 2, rows_each)]
-    across = [links.send(lat.at[h], lat_all.at[me, h], zl=1) for h in halves]
-    beside = links.send(lat, lat_all.at[me], core=1)
 
     def norm_rows(owner):
         def rows16(index, carry):
@@ -270,19 +295,22 @@
         lax.fori_loop(0, rows_each // 16, rows16, 0)
 
     own_lat.wait()
-    get_wt.wait()
-    for third in range(3):
-        here = slice(third * channels, (third + 1) * channels)
-        mod[:, here] = dot(embed, wt[:, here])
+    norm_rows(me)
     g_ws.relay()
-    g_ws.spread(True)
     g_1.spread(False)
-    g_2.along_z()
-    norm_rows(me)
     beside.wait_recv()
     norm_rows(beside_me)
+    g_ws.spread(True)
+    g_1.relay()
+
+    place_c = lanes_of(layout[...].astype(F32), tokens)
+    lane = lax.broadcasted_iota(jnp.int32, (tokens, 128), 1)
+    omega = jnp.exp(-math.log(10000.0) * (lane % 64).astype(F32) / 64)
+    tables[0] = jnp.cos(place_c * omega)
+    sine = jnp.sin(place_c * omega)
+    tables[1] = jnp.where(lane < 64, -sine, sine)
+
     g_ws.relay()
-    g_1.relay()
     g_1.spread(True)
     passed = []
     for copy, h in zip(across, halves):
@@ -318,13 +346,6 @@
     g_2.spread(True)
     lax.fori_loop(0, channels // 128, flip, 0)
 
-    place_c = lanes_of(layout[...].astype(F32), tokens)
-    lane = lax.broadcasted_iota(jnp.int32, (tokens, 128), 1)
-    omega = jnp.exp(-math.log(10000.0) * (lane % 64).astype(F32) / 64)
-    tables[0] = jnp.cos(place_c * omega)
-    sine = jnp.sin(place_c * omega)
-    tables[1] = jnp.where(lane < 64, -sine, sine)
-
     passed = []
     for index in range(2):
         rows = pl.ds(index * size, size)
@@ -348,6 +369,8 @@
             return carry
 
         lax.fori_loop(0, size // 16, rows16, 0)
+        if index == 0:
+            g_2.relay()
     g_1.settle()
 
     def project(head, source, base):
@@ -391,7 +414,6 @@
         dot(tnorm_b[...], wx_1_all[:, :, :, :, pl.ds(fold_at, 128)].reshape(channels, 128))
     )
     vrow[...] = (value_t[0:8] + value_t[8:16] + value_t[16:24]).astype(BF16).astype(F32)
-    g_2.relay()
     lax.fori_loop(0, early * blocks, attend, 0)
     g_2.settle()
     links.drain()
@@ -504,8 +526,8 @@
     stages = []
     for first_axis, second_axis, base in (("y", "x", 0), ("x", "y", 2)):
         big, spare = spare[:6], spare[6:]
-        small, spare = spare[:6], spare[6:]
-        mid, mid_b, spare = spare[0], spare[1], spare[2:]
+        inbox, mid, mid_b = spare[:3]
+        spare = spare[3:]
 
         def plain1(half, step, axis=first_axis, other=second_axis, base=base):
             return grads.at[slot_of(links, axis, step, other, base + half)]
@@ -516,11 +538,11 @@
         def spot_of(step, axis=second_axis):
             return ({"x": links.x, "y": links.y}[axis] + step) % 4
 
-        def plain2(half, step, mid_b=mid_b, spot=spot_of):
-            return mid_b.at[half, spot(step)]
-
-        def read2(half, step, mid=mid, spot=spot_of):
-            return mid[half, spot(step)]
+        def plain2(step, mid_b=mid_b, spot=spot_of):
+            return mid_b.at[:, spot(step)]
+
+        def read2(half, mid=mid, spot=spot_of):
+            return mid[half, spot(0)]
 
         stages.append(
             (
@@ -528,7 +550,7 @@
                 mid,
                 mid_b,
                 Scatter(links, first_axis, read1, plain1, big),
-                Scatter(links, second_axis, read2, plain2, small),
+                Direct(links, second_axis, read2, plain2, inbox),
             )
         )
     for quarter in (0, 2, 1, 3):
@@ -545,10 +567,7 @@
             mid_b[half] = value.astype(BF16)
 
         first_ring.finish(store)
-        second_ring.start(0)
-        second_ring.start(1)
-    for pair in stages:
-        pair[4].middle()
+        second_ring.start()
     for base, mid, mid_b, first_ring, second_ring in stages:
 
         def hold(half, value, base=base):
@@ -580,7 +599,7 @@
     wide = w_qk.shape[1] + 128
     narrow = (heads - 1) // 2 * 2 * HD + 128
     big = [VMEM((4, rows, cols), BF16)] * 4 + [VMEM((2, 4, rows, cols), BF16)] * 2
-    small = [VMEM((rows, cols), BF16)] * 4 + [VMEM((2, rows, cols), BF16)] * 2
+    small = [VMEM((3, 2, rows, cols), BF16)]
     mids = [VMEM((2, 4, rows, cols), F32), VMEM((2, 4, rows, cols), BF16)]
     scratch = [
         pltpu.SemaphoreType.DMA((128,)),
@@ -649,7 +668,7 @@
         compiler_params=pltpu.CompilerParams(
             collective_id=1, has_side_effects=True, vmem_limit_bytes=67043328
         ),
-    )(latents, noise, steps, layout, w_time, w_student, w_qk, w_value, w_disc.reshape(1, cols))
+    )(latents, noise, steps, layout, w_time, w_student, w_qk, w_value, w_disc)
     return (losses[0, : steps.shape[0]], student_grad)
 
 

time: 166 us -> 161 us (0.970)
  Pallas kernels: 161 us -> 156 us
    pallas_call x1, Pallas kernels: 161 us -> 156 us  [shards(): pl.pallas_call(step_body, out_shape=(jax.ShapeDtypeStruct((rows, cols), F...]
where the time goes in v4:
time: 161 us; the launch traced here: 159 us
  Pallas kernels  156 us (97%)
  local copies, waits for them, and re-layouts  2.72 us (2%)
    pallas_call x1, Pallas kernels, shards(): pl.pallas_call(step_body, out_shape=(jax.ShapeDtypeStruct((rows, cols), F...  156 us

profile of v4, /device:TPU:8, one launch (start us, length us, event | category | flops | bytes accessed | tf_op | source)
XLA Modules:
  0.0 159.3 jit_solution(1610962740058645651)
XLA Ops:
  0.6 156.0 %shard_map.104 = (f32[40,640]{1,0:T(8,128)}, f32[8,128]{1,0:T(8,128)}) custom-call(bf16[128,2560]{1,0:T(8,128)(2,1)} %lat.1, bf16[512,640]{1,0:T(8,128)(2,1)} %noise.1, s32[64]{0:T(128)} %steps.1, s32[1,512]{1,0:T(1,128)} %layout.1, bf16[256,7680]{1,0:T(8,128)(2,1)} %w_time.1, bf16[40,640]{1,0:T(8,128)(2,1)} %ws.1, bf16[40,1280]{1,0:T(8,128)(2,1)} %wqk.1, ...), custom_call_target="tpu_custom_call" | custom-call | tf_op jit(solution)/shard_map/pallas_call | solution.py:649
  156.6 1.2 slice_bitcast_fusion
  157.8 1.5 copy.12

commit v5 on v4

--- a/solution.py
+++ b/solution.py
@@ -108,20 +108,15 @@
         for first_axis, second_axis, base in AXES_AB:
             axis = second_axis if second else first_axis
             other = first_axis if second else None
-            mine = self.out.at[slot_of(links, axis, 0, other, slice(base, base + 2))]
-            self.near.append(
-                (
-                    axis,
-                    other,
-                    base,
-                    links.send(mine, mine, **{axis: 1}),
-                    links.send(mine, mine, **{axis: 3}),
-                )
-            )
+            half = [self.out.at[slot_of(links, axis, 0, other, base + i)] for i in range(2)]
+            up = links.send(half[0], half[0], **{axis: 1})
+            down = links.send(half[1], half[1], **{axis: 3})
+            self.near.append((axis, other, base, up, down))
+            self.copies.append(links.send(half[1], half[1], **{axis: 1}))
+            self.copies.append(links.send(half[0], half[0], **{axis: 3}))
 
     def relay(self):
         links = self.links
-        self.copies = []
         for axis, other, base, up, down in self.near:
             up.wait_recv()
             piece = self.out.at[slot_of(links, axis, 3, other, base)]
@@ -602,8 +597,8 @@
     small = [VMEM((3, 2, rows, cols), BF16)]
     mids = [VMEM((2, 4, rows, cols), F32), VMEM((2, 4, rows, cols), BF16)]
     scratch = [
-        pltpu.SemaphoreType.DMA((128,)),
-        pltpu.SemaphoreType.DMA((128,)),
+        pltpu.SemaphoreType.DMA((160,)),
+        pltpu.SemaphoreType.DMA((160,)),
         pltpu.SemaphoreType.DMA((5,)),
         VMEM(w_time.shape, BF16),
         VMEM((rows, narrow), BF16),

time: 161 us -> 155 us (0.963)
  Pallas kernels: 156 us -> 151 us
    pallas_call x1, Pallas kernels: 156 us -> 151 us  [shards(): pl.pallas_call(step_body, out_shape=(jax.ShapeDtypeStruct((rows, cols), F...]
where the time goes in v5:
time: 155 us
  Pallas kernels  151 us (97%)
  local copies, waits for them, and re-layouts  2.72 us (2%)
    pallas_call x1, Pallas kernels, shards(): pl.pallas_call(step_body, out_shape=(jax.ShapeDtypeStruct((rows, cols), F...  151 us

profile of v5, /device:TPU:8, one launch (start us, length us, event | category | flops | bytes accessed | tf_op | source)
XLA Modules:
  0.0 154.8 jit_solution(9610291071430378129)
XLA Ops:
  0.6 151.4 %shard_map.104 = (f32[40,640]{1,0:T(8,128)}, f32[8,128]{1,0:T(8,128)}) custom-call(bf16[128,2560]{1,0:T(8,128)(2,1)} %lat.1, bf16[512,640]{1,0:T(8,128)(2,1)} %noise.1, s32[64]{0:T(128)} %steps.1, s32[1,512]{1,0:T(1,128)} %layout.1, bf16[256,7680]{1,0:T(8,128)(2,1)} %w_time.1, bf16[40,640]{1,0:T(8,128)(2,1)} %ws.1, bf16[40,1280]{1,0:T(8,128)(2,1)} %wqk.1, ...), custom_call_target="tpu_custom_call" | custom-call | tf_op jit(solution)/shard_map/pallas_call | solution.py:644
  152.1 1.2 slice_bitcast_fusion
  153.3 1.5 copy.12

commit v6 on v5

--- a/solution.py
+++ b/solution.py
@@ -484,10 +484,9 @@
 
     pieces = [pl.ds(index * size, size) for index in range(2)]
     first, second, third = [], [], []
-    for rows in pieces:
+    for index, rows in enumerate(pieces):
         stage[1, rows] = d_block(far_beside, rows).astype(BF16)
         first.append(links.send(stage.at[1, rows], from_core.at[1, rows], core=1))
-    for index, rows in enumerate(pieces):
         value = d_block(far, rows)
         first[index].wait_recv()
         cross[rows] = (value + from_core[1, rows].astype(F32)).astype(BF16)

time: 155 us -> 155 us (level)
  no operation moved by 1% of the time
where the time goes in v6:
time: 155 us; the launch traced here: 154 us
  Pallas kernels  151 us (97%)
  local copies, waits for them, and re-layouts  2.72 us (2%)
    pallas_call x1, Pallas kernels, shards(): pl.pallas_call(step_body, out_shape=(jax.ShapeDtypeStruct((rows, cols), F...  151 us

profile of v6, /device:TPU:8, one launch (start us, length us, event | category | flops | bytes accessed | tf_op | source)
XLA Modules:
  0.0 154.2 jit_solution(6539879815473238269)
XLA Ops:
  0.6 150.8 %shard_map.104 = (f32[40,640]{1,0:T(8,128)}, f32[8,128]{1,0:T(8,128)}) custom-call(bf16[128,2560]{1,0:T(8,128)(2,1)} %lat.1, bf16[512,640]{1,0:T(8,128)(2,1)} %noise.1, s32[64]{0:T(128)} %steps.1, s32[1,512]{1,0:T(1,128)} %layout.1, bf16[256,7680]{1,0:T(8,128)(2,1)} %w_time.1, bf16[40,640]{1,0:T(8,128)(2,1)} %ws.1, bf16[40,1280]{1,0:T(8,128)(2,1)} %wqk.1, ...), custom_call_target="tpu_custom_call" | custom-call | tf_op jit(solution)/shard_map/pallas_call | solution.py:643
  151.4 1.2 slice_bitcast_fusion
  152.6 1.5 %copy.12 = f32[40,640]{1,0:T(8,128)} copy(f32[40,640]{1,0:T(8,128)} %get-tuple-element.9) | data formatting | bytes 204800
